TPU v7x, 128 devices: a whole 4x4x4 slice. The times are simulated.
128 devices in a mesh: gx: 32 (over z, y, core), gy: 4 (over x).
Axes of the slice: x: 4, y: 4, z: 4, core: 2. Of those that a mesh axis runs over, the one named last changes fastest.
Arguments:
- tokens: bfloat16 [512, 9216], P(('gx', 'gy')), may hold values from -6 to 6
- gain: float32 [9216], replicated, may hold values from 0.1 to 1.9
- w_gate: bfloat16 [9216, 36864], P('gy', 'gx'), may hold values from -0.0625 to 0.0625
- w_up: bfloat16 [9216, 36864], P('gy', 'gx'), may hold values from -0.0625 to 0.0625
- w_down: bfloat16 [36864, 9216], P('gx', 'gy'), may hold values from -0.03125 to 0.03125
- w_kv: bfloat16 [4, 2304, 512], P('gy', 'gx'), may hold values from -0.0625 to 0.0625
- queries: bfloat16 [512, 12288], P(('gx', 'gy')), may hold values from -64 to 64
- key_cache: bfloat16 [512, 2048, 256], P(('gx', 'gy')), may hold values from -4 to 4
- value_cache: bfloat16 [512, 2048, 256], P(('gx', 'gy')), may hold values from -6 to 6
- lengths: int32 [512], P(('gx', 'gy')), may hold values from 2 to 2048, as said below
Outputs:
- mixed: bfloat16 [512, 9216], P(('gx', 'gy'))
- context: bfloat16 [512, 12288], P(('gx', 'gy'))
Inputs may be any that keep to these rules, and one draw needn't show every extreme that they name: `lengths`: each row has at least two live slots, and some row fills all 2048 slots.
All inputs are finite; a program needn't handle non-finite values.
Results may differ from a plain program's by a relative error of at most 0.0055.
Values may be sent and summed in bfloat16 or wider, within the bound.
A program may use at most 128 MiB of HBM per device.

v0:
```python
import math

import jax
import jax.numpy as jnp
from jax import lax
from jax.sharding import PartitionSpec as P

HD = 256


def layer_norm(tokens, gain):
    values = tokens.astype(jnp.float32)
    centred = values - jnp.mean(values, axis=-1, keepdims=True)
    spread = jnp.mean(centred * centred, axis=-1, keepdims=True)
    return (centred * lax.rsqrt(spread + 1e-05) * gain).astype(jnp.bfloat16)


def gated(pair, hidden_cols):
    return (jax.nn.silu(pair[:, :hidden_cols]) * pair[:, hidden_cols:]).astype(jnp.bfloat16)


def attend(queries, key_cache, value_cache, lengths, key_new, value_new):
    batch = queries.shape[0]
    span = key_cache.shape[1]
    depth = key_cache.shape[2]
    grouped = queries.reshape(batch, -1, depth)
    scale = 1.0 / math.sqrt(depth)
    scores = (
        jnp.einsum("rhd,rcd->rhc", grouped, key_cache, preferred_element_type=jnp.float32) * scale
    )
    own = jnp.einsum("rhd,rd->rh", grouped, key_new, preferred_element_type=jnp.float32) * scale
    live = lax.broadcasted_iota(jnp.int32, (batch, span), 1) < lengths[:, None]
    scores = jnp.where(live[:, None, :], scores, -jnp.inf)
    top = jnp.maximum(jnp.max(scores, axis=-1), own)
    weights = jnp.exp(scores - top[:, :, None])
    own_weight = jnp.exp(own - top)
    total = jnp.sum(weights, axis=-1) + own_weight
    probs = (weights / total[:, :, None]).astype(jnp.bfloat16)
    own_prob = (own_weight / total).astype(jnp.bfloat16)
    context = jnp.einsum("rhc,rcd->rhd", probs, value_cache, preferred_element_type=jnp.float32)
    context = (
        context
        + own_prob.astype(jnp.float32)[:, :, None] * value_new.astype(jnp.float32)[:, None, :]
    )
    return context.reshape(batch, -1).astype(jnp.bfloat16)


def body(tokens, gain, w_gate, w_up, w_down, w_kv, queries, key_cache, value_cache, lengths):
    normed = layer_norm(tokens, gain)
    grid_in = lax.all_to_all(normed, "gy", split_axis=1, concat_axis=0, tiled=True)
    slab = w_kv.shape[1]
    offset = lax.axis_index("gx") * slab
    hidden_cols = w_gate.shape[1]
    piece = lax.all_gather(grid_in, "gx", axis=0, tiled=True)
    part_cols = lax.dynamic_slice_in_dim(piece, offset, slab, 1)
    partial_value = jnp.concatenate(
        (
            jnp.dot(piece, w_gate, preferred_element_type=jnp.float32),
            jnp.dot(piece, w_up, preferred_element_type=jnp.float32),
            jnp.dot(part_cols, w_kv[0], preferred_element_type=jnp.float32),
        ),
        axis=1,
    )
    pair = partial_value[:, : 2 * hidden_cols]
    kv_term = partial_value[:, 2 * hidden_cols :]
    summed = lax.psum(pair, "gy")
    hidden = gated(summed, hidden_cols)
    back = lax.psum_scatter(
        jnp.concatenate(
            (jnp.dot(hidden, w_down, preferred_element_type=jnp.float32), kv_term), axis=1
        ),
        "gx",
        scatter_dimension=0,
        tiled=True,
    )
    width_dev = w_down.shape[1]
    ffn, kv_sums = (
        lax.all_to_all(back[:, :width_dev], "gy", split_axis=0, concat_axis=1, tiled=True),
        lax.all_to_all(back[:, width_dev:], "gy", split_axis=0, concat_axis=1, tiled=True),
    )
    fresh = jnp.sum(kv_sums.reshape(kv_sums.shape[0], -1, 2 * HD), axis=1)
    mixed = (tokens.astype(jnp.float32) + ffn).astype(jnp.bfloat16)
    key_new = fresh[:, :HD].astype(jnp.bfloat16)
    value_new = fresh[:, HD:].astype(jnp.bfloat16)
    context = attend(queries, key_cache, value_cache, lengths, key_new, value_new)
    return (mixed, context)


def solution(mesh):
    return jax.shard_map(
        body,
        mesh=mesh,
        in_specs=(
            P(("gx", "gy"), None),
            P(),
            P("gy", "gx"),
            P("gy", "gx"),
            P("gx", "gy"),
            P("gy", "gx", None),
            P(("gx", "gy"), None),
            P(("gx", "gy"), None, None),
            P(("gx", "gy"), None, None),
            P(("gx", "gy")),
        ),
        out_specs=(P(("gx", "gy"), None), P(("gx", "gy"), None)),
        check_vma=False,
    )
```

profile of v0, /device:TPU:1, one launch (start us, length us, event | category | flops | bytes accessed | tf_op | source)
XLA Modules:
  0.0 302.2 jit_solution(14279376726392762262)
XLA Ops:
  7.2 1.1 convert_reduce_fusion
  8.3 1.1 fusion.12
  9.5 1.0 fusion.14
  10.5 9.2 %all_to_all.51 = bf16[4,4,2304]{2,0,1:T(4,128)(2,1)S(1)} all-to-all(bf16[4,4,2304]{2,0,1:T(4,128)(2,1)S(1)} %bitcast.32), channel_id=1, replica_groups=mesh['gx'=32,'gy'=4] {'gy'}, dimensions={1} | all-to-all | bytes 147456 | tf_op jit(solution)/shard_map/all_to_all | solution.py:50
  19.6 0.7 all_to_all.41
  20.4 46.8 %all-gather.2.cloned.1.call-done = bf16[512,2304]{1,0:T(8,128)(2,1)} async-done(((bf16[16,2304]{1,0:T(8,128)(2,1)}), bf16[512,2304]{1,0:T(8,128)(2,1)}) %all-gather.2.cloned.1.call-update) | async-done | bytes 2359312 | tf_op jit(solution)/shard_map/all_gather | solution.py:54
  67.2 6.6 %fusion.30 = f32[512,1152]{1,0:T(8,128)S(1)} fusion(bf16[512,2304]{1,0:T(8,128)(2,1)} %all-gather.2.cloned.1.call-done, bf16[2304,1152]{1,0:T(8,128)(2,1)} %param.12), kind=kOutput, calls=%fused_computation.47 | convolution fusion | flops 2717908992 | bytes 10027008 | tf_op jit(solution)/shard_map/dot_general | solution.py:58
  73.8 5.8 %fusion.31 = f32[512,1152]{1,0:T(8,128)S(1)} fusion(bf16[512,2304]{1,0:T(8,128)(2,1)S(1)} %copy-done.3, bf16[2304,1152]{1,0:T(8,128)(2,1)} %param.13), kind=kOutput, calls=%fused_computation.48 | convolution fusion | flops 2717908992 | bytes 10027008 | tf_op jit(solution)/shard_map/dot_general | solution.py:59
  79.6 2.5 pad_maximum_fusion.1
  82.5 99.8 %all-reduce.2.cloned.1.call-done = f32[512,2304]{1,0:T(8,128)} async-done(((f32[512,2304]{1,0:T(8,128)}), f32[512,2304]{1,0:T(8,128)}) %all-reduce.2.cloned.1.call-update) | async-done | bytes 4718608 | tf_op jit(solution)/shard_map/psum | solution.py:66
  182.4 6.9 %fusion.3 = f32[512,2304]{1,0:T(8,128)S(1)} fusion(bf16[1152,2304]{1,0:T(8,128)(2,1)} %param.14, f32[512,2304]{1,0:T(8,128)} %all-reduce.2.cloned.1.call-done), kind=kOutput, calls=%fused_computation.9 | convolution fusion | flops 2721447936 | bytes 14745600 | tf_op jit(solution)/shard_map/dot_general | solution.py:70
  189.3 2.9 pad_maximum_fusion
  192.2 0.6 copy-done.4
  192.9 83.2 %reduce-scatter.2.cloned.1.call-done = f32[16,2816]{1,0:T(8,128)} async-done(((f32[512,2816]{1,0:T(8,128)}), f32[16,2816]{1,0:T(8,128)}) %reduce-scatter.2.cloned.1.call-update) | async-done | bytes 180240 | tf_op jit(solution)/shard_map/reduce_scatter | solution.py:68
  276.1 0.8 slice.29
  276.9 0.6 all_to_all.46
  277.5 4.0 %all-to-all-start.2 = ((f32[4,4,512]{2,1,0:T(4,128)}), f32[4,4,512]{2,1,0:T(4,128)S(1)}, u32[]{:S(2)}, u32[]{:S(2)}) async-start(f32[4,4,512]{2,1,0:T(4,128)} %all_to_all.46), calls=%async_computation.3 | async-start | bytes 65536 | tf_op jit(solution)/shard_map/all_to_all | solution.py:79
  281.5 3.7 %fusion.29 = (f32[4,48]{1,0:T(4,128)S(1)}, f32[4,48,2048]{2,1,0:T(8,128)S(1)}) fusion(bf16[4,2048,256]{2,1,0:T(8,128)(2,1)} %param.17, bf16[1,4,48,256]{3,1,2,0:T(4,128)(2,1)S(1)} %bitcast.34, pred[4,2048]{1,0:T(4,128)(4,1)S(1)} %iota_compare_fusion), kind=kOutput, calls=%fused_computation.46 | convolution fusion | flops 202506048 | bytes 5874432 | tf_op jit(solution)/shard_map/rhd,rcd->rhc/dot_general | solution.py:29
  285.1 0.7 all_to_all.42
  285.8 4.2 %all-to-all-start.1 = ((f32[4,4,2304]{2,1,0:T(4,128)}), f32[4,4,2304]{2,1,0:T(4,128)S(1)}, u32[]{:S(2)}, u32[]{:S(2)}) async-start(f32[4,4,2304]{2,1,0:T(4,128)} %all_to_all.42), calls=%async_computation.2 | async-start | bytes 294912 | tf_op jit(solution)/shard_map/all_to_all | solution.py:78
  290.7 3.1 %fusion.7 = bf16[1,4,48,256]{3,2,1,0:T(8,128)(2,1)S(1)} fusion(bf16[4,2048,256]{2,1,0:T(8,128)(2,1)} %param.18, f32[4,48,2048]{2,1,0:T(8,128)S(1)} %get-tuple-element.7, f32[4,48]{1,0:T(4,128)S(1)} %get-tuple-element.3, f32[4,48]{1,0:T(4,128)S(1)} %multiply_maximum_fusion, f32[4,256]{1,0:T(4,128)S(1)} %get-tuple-element.4, f32[4,48]{1,0:T(4,128)S(1)} %get-tuple-element.2), kind=kOutput, calls=%fused_computation.13 | convolution fusion | flops 202653696 | bytes 5871872 | tf_op jit(solution)/shard_map/rhc,rcd->rhd/dot_general | solution.py:40
  293.8 0.7 copy.21
  294.5 0.5 all-to-all-done.1
  295.0 0.7 fusion.15
  (28 shorter events, 1.2 us)
Async XLA Ops:
  7.2 75.0 %copy-start = (bf16[1,72,512]{2,1,0:T(8,128)(2,1)S(1)}, bf16[1,72,512]{2,1,0:T(8,128)(2,1)}, u32[]{:S(2)}) copy-start(bf16[1,72,512]{2,1,0:T(8,128)(2,1)} %param.15) | copy-start | bytes 221188
  7.2 60.0 %all-gather.2.cloned.1.call-start = ((), (), s32[]{:S(2)}) async-start(), calls=%async_computation.4 | async-start | bytes 2433024 | tf_op jit(solution)/shard_map/all_gather | solution.py:54
  20.3 162.0 %all-reduce.2.cloned.1.call-start = ((), (), s32[]{:S(2)}) async-start(), calls=%async_computation.5 | async-start | bytes 9437184 | tf_op jit(solution)/shard_map/psum | solution.py:66
  67.2 6.6 %copy-start.3 = (bf16[512,2304]{1,0:T(8,128)(2,1)S(1)}, bf16[512,2304]{1,0:T(8,128)(2,1)}, u32[]{:S(2)}) copy-start(bf16[512,2304]{1,0:T(8,128)(2,1)} %all-gather.2.cloned.1.call-done) | copy-start | bytes 7077892
  82.1 194.0 %reduce-scatter.2.cloned.1.call-start = ((), (), s32[]{:S(2)}) async-start(), calls=%async_computation.6 | async-start | bytes 5947392 | tf_op jit(solution)/shard_map/reduce_scatter | solution.py:68
  192.2 0.7 copy-start.4
  192.2 89.3 %copy-start.2 = (bf16[4,12288]{1,0:T(4,128)(2,1)S(1)}, bf16[4,12288]{1,0:T(4,128)(2,1)}, u32[]{:S(2)}) copy-start(bf16[4,12288]{1,0:T(4,128)(2,1)} %param.16) | copy-start | bytes 294916
  277.5 8.4 %all-to-all-start.2 = ((f32[4,4,512]{2,1,0:T(4,128)}), f32[4,4,512]{2,1,0:T(4,128)S(1)}, u32[]{:S(2)}, u32[]{:S(2)}) async-start(f32[4,4,512]{2,1,0:T(4,128)} %all_to_all.46), calls=%async_computation.3 | async-start | bytes 65536 | tf_op jit(solution)/shard_map/all_to_all | solution.py:79
  281.5 3.7 %slice-start = ((f32[16,2816]{1,0:T(8,128)}), f32[16,2304]{1,0:T(8,128)S(1)}, s32[]{:S(2)}) async-start(f32[16,2816]{1,0:T(8,128)} %reduce-scatter.2.cloned.1.call-done), calls=%async_computation.7 | async-start | bytes 294912 | tf_op jit(solution)/shard_map/slice | solution.py:78
  285.8 9.2 %all-to-all-start.1 = ((f32[4,4,2304]{2,1,0:T(4,128)}), f32[4,4,2304]{2,1,0:T(4,128)S(1)}, u32[]{:S(2)}, u32[]{:S(2)}) async-start(f32[4,4,2304]{2,1,0:T(4,128)} %all_to_all.42), calls=%async_computation.2 | async-start | bytes 294912 | tf_op jit(solution)/shard_map/all_to_all | solution.py:78
  290.6 4.4 %copy-start.1 = (bf16[4,9216]{1,0:T(4,128)(2,1)S(1)}, bf16[4,9216]{1,0:T(4,128)(2,1)}, u32[]{:S(2)}) copy-start(bf16[4,9216]{1,0:T(4,128)(2,1)} %param.10) | copy-start | bytes 221188
Sparse Core Ops, SparseCore 0:
  20.4 46.7 all-gather.1
  82.2 100.0 all-reduce.1
  192.3 83.7 reduce-scatter.1
where the time goes:
time: 306 us; the launch traced here: 302 us
  waiting for transfers between devices  230 us (75%)
  matrix products  26.5 us (9%)
  between operations  13.8 us (5%)
  other arithmetic  9.81 us (3%)
  blocking collectives  9.16 us (3%)
  starting transfers between devices  8.33 us (3%)
  local copies, waits for them, and re-layouts  4.08 us (1%)
    psum x1, waiting for transfers between devices, body(): summed = lax.psum(pair, 'gy')  99.8 us
    reduce_scatter x1, waiting for transfers between devices, body(): lax.psum_scatter(jnp.concatenate((jnp.dot(hidden, w_down, preferred_eleme...  83.2 us
    all_gather x1, waiting for transfers between devices, body(): piece = lax.all_gather(grid_in, 'gx', axis=0, tiled=True)  46.8 us
    all_to_all x1, blocking collectives, body(): lax.all_to_all(normed, 'gy', split_axis=1, concat_axis=0, tiled=True)  9.16 us
    dot_general x1, matrix products, body(): jnp.dot(hidden, w_down, preferred_element_type=jnp.float32)  6.92 us
    dot_general x1, matrix products, body(): jnp.dot(piece, w_gate, preferred_element_type=jnp.float32)  6.57 us
  transfers between devices with their start and end apart: 5, of which 4 were waited for; matrix products, arithmetic and copies ran while one was open for 3% of the time, Pallas kernels for 0%

commit v1 on v0

v1 whole, which is shorter than its diff:
```python
import functools
import math

import jax
import jax.numpy as jnp
from jax import lax
from jax.experimental import pallas as pl
from jax.experimental.pallas import tpu as pltpu
from jax.sharding import PartitionSpec as P

MESH = pl.DeviceIdType.MESH
HD = 256
HEADS = 48
NZ, NY, NC, NX = 4, 4, 2, 4
SLAB = 16
TILE = 128
GRAN = 3
F32 = jnp.float32
BF16 = jnp.bfloat16


def step_kernel(
    tokens_ref, gain_ref, q_ref, len_ref, wkv_ref,
    wg_hbm, wu_hbm, wd_hbm, k_hbm, v_hbm,
    mixed_ref, ctx_ref,
    kbuf, vbuf, wgu, wd, nx, xr, xa, wpad, kp, kr, ks, kzr, kyr, kts, kt2r, kx, kxr,
    ps, rv, hs, dp, dr, ds_, azr, byr, ta, tb, tar, tbr, fx, fxr,
    m_s, l_s, acc_s, ssem, rsem, lsem,
):
    d_dev = xa.shape[-1]
    half = d_dev // 2
    gx = lax.axis_index("gx")
    x = lax.axis_index("gy")
    z = gx // (NY * NC)
    y = lax.rem(gx // NC, NY)
    c = lax.rem(gx, NC)
    oc = 1 - c

    def dev(dz=0, dy=0, dc=0, dx=0):
        zz, yy, cc = lax.rem(z + dz, NZ), lax.rem(y + dy, NY), lax.rem(c + dc, NC)
        return ((zz * NY + yy) * NC + cc, lax.rem(x + dx, NX))

    counter = [0]
    sent = []

    def rcopy(src, dst, device):
        i = counter[0]
        counter[0] += 1
        cp = pltpu.make_async_remote_copy(
            src_ref=src, dst_ref=dst, send_sem=ssem.at[i], recv_sem=rsem.at[i],
            device_id=device, device_id_type=MESH,
        )
        cp.start()
        sent.append(cp)
        return cp

    bar = pltpu.get_barrier_semaphore()
    peers = (
        [dev(dz=i) for i in range(1, NZ)] + [dev(dy=i) for i in range(1, NY)]
        + [dev(dx=i) for i in range(1, NX)] + [dev(dc=1)]
    )
    for peer in peers:
        pl.semaphore_signal(bar, inc=1, device_id=peer, device_id_type=MESH)

    kcp = [pltpu.make_async_copy(k_hbm.at[r], kbuf.at[r], lsem.at[0, r]) for r in range(4)]
    vcp = [pltpu.make_async_copy(v_hbm.at[r], vbuf.at[r], lsem.at[1, r]) for r in range(4)]
    for r in range(4):
        kcp[r].start()
        vcp[r].start()
    n_tiles = wgu.shape[0]

    def weight_copies(t):
        cols = pl.ds(pl.multiple_of(t * TILE, TILE), TILE)
        return (
            pltpu.make_async_copy(wg_hbm.at[:, cols], wgu.at[t, :, pl.ds(0, TILE)], lsem.at[2, t]),
            pltpu.make_async_copy(wu_hbm.at[:, cols], wgu.at[t, :, pl.ds(TILE, TILE)], lsem.at[3, t]),
        )

    for t in range(n_tiles):
        for cp in weight_copies(t):
            cp.start()
    wdcp = pltpu.make_async_copy(wd_hbm, wd, lsem.at[4, 0])
    wdcp.start()

    values = tokens_ref[...].astype(F32)
    centred = values - jnp.mean(values, axis=-1, keepdims=True)
    spread = jnp.mean(centred * centred, axis=-1, keepdims=True)
    normed = centred * lax.rsqrt(spread + 1e-05) * gain_ref[...]
    for j in range(NX):
        nx[j] = normed[:, j * d_dev : (j + 1) * d_dev]

    pl.semaphore_wait(bar, len(peers))

    cps = [
        rcopy(nx.at[lax.rem(x + i, NX)], xr.at[x], dev(dx=i)) for i in range(1, NX)
    ]
    xr[x] = nx[x]
    for cp in cps:
        cp.wait_recv()
    xa[c, z, y] = jnp.concatenate([xr[j] for j in range(NX)], axis=0).astype(BF16)

    ca, cb = pl.ds(0, half), pl.ds(half, half)
    st1 = [
        rcopy(xa.at[c, z, y, :, ca], xa.at[c, z, y, :, ca], dev(dy=i)) for i in range(1, NY)
    ] + [
        rcopy(xa.at[c, z, y, :, cb], xa.at[c, z, y, :, cb], dev(dz=i)) for i in range(1, NZ)
    ]

    scale = 1.0 / math.sqrt(HD)

    def attend(r):
        s = lax.dot_general(
            q_ref[r], kbuf[r], (((1,), (1,)), ((), ())), preferred_element_type=F32
        ) * scale
        live = lax.broadcasted_iota(jnp.int32, s.shape, 1) < len_ref[r]
        s = jnp.where(live, s, -jnp.inf)
        m = jnp.max(s, axis=-1, keepdims=True)
        p = jnp.exp(s - m)
        l = jnp.sum(p, axis=-1, keepdims=True)
        m_s[r] = jnp.broadcast_to(m, m_s.shape[1:])
        l_s[r] = jnp.broadcast_to(l, l_s.shape[1:])
        acc_s[r] = jnp.dot(p.astype(BF16), vbuf[r], preferred_element_type=F32)

    kcp[0].wait()
    vcp[0].wait()
    attend(0)

    for cp in st1:
        cp.wait_recv()
    st2 = [
        rcopy(xa.at[c, z, :, :, ca], xa.at[c, z, :, :, ca], dev(dz=i)) for i in range(1, NZ)
    ] + [
        rcopy(xa.at[c, :, y, :, cb], xa.at[c, :, y, :, cb], dev(dy=i)) for i in range(1, NY)
    ]
    for r in range(1, 4):
        kcp[r].wait()
        vcp[r].wait()
    lax.fori_loop(1, 4, lambda r, _: (attend(r), 0)[1], 0)

    span = wkv_ref.shape[0]
    offset = gx * span
    start = jnp.minimum(offset // TILE, d_dev // TILE - 2) * TILE
    wide = jnp.concatenate(
        [wkv_ref[...].astype(F32), jnp.zeros((2 * TILE - span, 2 * HD), F32)], axis=0
    )
    wpad[...] = pltpu.roll(wide, offset - start, axis=0).astype(BF16)

    for cp in st2:
        cp.wait_recv()
    sib = rcopy(xa.at[c], xa.at[c], dev(dc=1))
    sib.wait_recv()

    rows = NC * NZ * NY * SLAB

    def reduce_core(part, other, out, cols):
        def add(i, _):
            a, b = i // NY, lax.rem(i, NY)
            out[a, b] = (part[c, a, b].astype(F32) + other[a, b].astype(F32)).astype(out.dtype)
            return 0

        lax.fori_loop(0, NZ * NY, add, 0)

    def reduce_first(out, az, by, ha, hb):
        return [
            rcopy(out.at[lax.rem(z + i, NZ), :, :, ha], az.at[i - 1], dev(dz=i)) for i in range(1, NZ)
        ] + [
            rcopy(out.at[:, lax.rem(y + i, NY), :, hb], by.at[i - 1], dev(dy=i)) for i in range(1, NY)
        ]

    def reduce_second(out, az, by, ta, tb, tar, tbr, ha, hb):
        def add_a(b, _):
            total = out[z, b, :, ha].astype(F32)
            for i in range(NZ - 1):
                total += az[i, b].astype(F32)
            ta[b] = total.astype(ta.dtype)
            return 0

        def add_b(a, _):
            total = out[a, y, :, hb].astype(F32)
            for i in range(NY - 1):
                total += by[i, a].astype(F32)
            tb[a] = total.astype(tb.dtype)
            return 0

        lax.fori_loop(0, NY, add_a, 0)
        cps = [rcopy(ta.at[lax.rem(y + i, NY)], tar.at[i - 1], dev(dy=i)) for i in range(1, NY)]
        lax.fori_loop(0, NZ, add_b, 0)
        return cps + [rcopy(tb.at[lax.rem(z + i, NZ)], tbr.at[i - 1], dev(dz=i)) for i in range(1, NZ)]

    def reduce_last(ta, tb, tar, tbr):
        a, b = ta[y].astype(F32), tb[z].astype(F32)
        for i in range(NY - 1):
            a += tar[i].astype(F32)
        for i in range(NZ - 1):
            b += tbr[i].astype(F32)
        return a, b

    xwin = xa[:, :, :, :, pl.ds(pl.multiple_of(start, TILE), 2 * TILE)].reshape(rows, 2 * TILE)
    kp[...] = jnp.dot(xwin, wpad[...], preferred_element_type=F32).reshape(kp.shape)
    ka, kb = pl.ds(0, HD), pl.ds(HD, HD)
    kv_core = rcopy(kp.at[oc], kr, dev(dc=1))

    per = n_tiles // GRAN
    chunk = rows // NX

    def gate_up(g):
        def tile(t, _):
            col = pl.ds(pl.multiple_of(t * 2 * TILE, 2 * TILE), 2 * TILE)
            for cp in weight_copies(g * per + t):
                cp.wait()
            part = jnp.dot(
                xa[...].reshape(rows, d_dev), wgu[g * per + t], preferred_element_type=F32
            )
            for k in range(NX):
                ps[k, g, :, col] = part[k * chunk : (k + 1) * chunk].astype(BF16)
            return 0

        lax.fori_loop(0, per, tile, 0)
        return [
            rcopy(ps.at[lax.rem(x + i, NX), g], rv.at[i - 1, g], dev(dx=i)) for i in range(1, NX)
        ]

    def activate(g, cps):
        for cp in cps:
            cp.wait_recv()
        for t in range(per):
            col = pl.ds(t * 2 * TILE, 2 * TILE)
            total = ps[x, g, :, col].astype(F32)
            for i in range(NX - 1):
                total += rv[i, g, :, col].astype(F32)
            gate, up = total[:, :TILE], total[:, TILE:]
            hs[x, :, pl.ds((g * per + t) * TILE, TILE)] = (
                gate / (1.0 + jnp.exp(-gate)) * up
            ).astype(BF16)
        cols = pl.ds(g * per * TILE, per * TILE)
        return [rcopy(hs.at[x, :, cols], hs.at[x, :, cols], dev(dx=i)) for i in range(1, NX)]

    g0 = gate_up(0)
    kv_core.wait_recv()
    reduce_core(kp, kr, ks, 2 * HD)
    kv1 = reduce_first(ks, kzr, kyr, ka, kb)
    g1 = gate_up(1)
    for cp in kv1:
        cp.wait_recv()
    kv2 = reduce_second(
        ks, kzr, kyr, kts.at[0], kts.at[1], kt2r.at[0], kt2r.at[1], ka, kb
    )
    g2 = gate_up(2)
    for cp in kv2:
        cp.wait_recv()
    key_sum, value_sum = reduce_last(kts.at[0], kts.at[1], kt2r.at[0], kt2r.at[1])
    for j in range(NX):
        kx[j] = jnp.concatenate([key_sum[4 * j : 4 * j + 4], value_sum[4 * j : 4 * j + 4]], axis=1)
    kv3 = [rcopy(kx.at[lax.rem(x + i, NX)], kxr.at[i - 1], dev(dx=i)) for i in range(1, NX)]
    h0 = activate(0, g0)
    for cp in kv3:
        cp.wait_recv()
    fresh = kx[x]
    for i in range(NX - 1):
        fresh += kxr[i]
    fresh = fresh.astype(BF16).astype(F32)
    for r in range(4):
        key_new, value_new = fresh[r : r + 1, :HD], fresh[r : r + 1, HD:]
        s_new = jnp.sum(q_ref[r].astype(F32) * key_new, axis=-1, keepdims=True) * scale
        m_old = m_s[r][:, :1]
        m = jnp.maximum(m_old, s_new)
        keep, own = jnp.exp(m_old - m), jnp.exp(s_new - m)
        total = l_s[r][:, :1] * keep + own
        prob = (own / total).astype(BF16).astype(F32)
        ctx_ref[r] = (acc_s[r] * (keep / total) + prob * value_new).astype(BF16)
    h1 = activate(1, g1)
    h2 = activate(2, g2)
    wdcp.wait()
    for cp in h0 + h1 + h2:
        cp.wait_recv()

    def down(t, _):
        col = pl.ds(pl.multiple_of(t * 256, 256), 256)
        part = jnp.dot(hs[...].reshape(rows, -1), wd[:, col], preferred_element_type=F32)
        dp[:, :, :, :, col] = part.astype(BF16).reshape(NC, NZ, NY, SLAB, 256)
        return 0

    lax.fori_loop(0, d_dev // 256, down, 0)
    core = rcopy(dp.at[oc], dr, dev(dc=1))
    core.wait_recv()
    reduce_core(dp, dr, ds_, d_dev)
    r1 = reduce_first(ds_, azr, byr, ca, cb)
    for cp in r1:
        cp.wait_recv()
    r2 = reduce_second(ds_, azr, byr, ta, tb, tar, tbr, ca, cb)
    for cp in r2:
        cp.wait_recv()
    low, high = reduce_last(ta, tb, tar, tbr)
    for j in range(NX):
        fx[j, :, ca] = low[4 * j : 4 * j + 4]
        fx[j, :, cb] = high[4 * j : 4 * j + 4]
    r3 = [rcopy(fx.at[lax.rem(x + i, NX)], fxr.at[x], dev(dx=i)) for i in range(1, NX)]
    fxr[x] = fx[x]
    for cp in r3:
        cp.wait_recv()
    for j in range(NX):
        cols = pl.ds(j * d_dev, d_dev)
        mixed_ref[:, cols] = (tokens_ref[:, cols].astype(F32) + fxr[j]).astype(BF16)
    for cp in sent:
        cp.wait_send()


def body(tokens, gain, w_gate, w_up, w_down, w_kv, queries, key_cache, value_cache, lengths):
    batch, width = tokens.shape
    d_dev, hid = w_gate.shape
    span = key_cache.shape[1]
    n_tiles = hid // TILE
    rows = NC * NZ * NY * SLAB
    chunk = rows // NX
    half = d_dev // 2
    per = n_tiles // GRAN
    vm = pl.BlockSpec(memory_space=pltpu.VMEM)
    hbm = pl.BlockSpec(memory_space=pltpu.HBM)
    mixed, context = pl.pallas_call(
        step_kernel,
        name="step",
        out_shape=(
            jax.ShapeDtypeStruct((batch, width), BF16),
            jax.ShapeDtypeStruct((batch, HEADS, HD), BF16),
        ),
        in_specs=[vm, vm, vm, pl.BlockSpec(memory_space=pltpu.SMEM), vm] + [hbm] * 5,
        out_specs=(vm, vm),
        scratch_shapes=[
            pltpu.VMEM((batch, span, HD), BF16),
            pltpu.VMEM((batch, span, HD), BF16),
            pltpu.VMEM((n_tiles, d_dev, 2 * TILE), BF16),
            pltpu.VMEM((hid, d_dev), BF16),
            pltpu.VMEM((NX, 4, d_dev), F32),
            pltpu.VMEM((NX, 4, d_dev), F32),
            pltpu.VMEM((NC, NZ, NY, SLAB, d_dev), BF16),
            pltpu.VMEM((2 * TILE, 2 * HD), BF16),
            pltpu.VMEM((NC, NZ, NY, SLAB, 2 * HD), F32),
            pltpu.VMEM((NZ, NY, SLAB, 2 * HD), F32),
            pltpu.VMEM((NZ, NY, SLAB, 2 * HD), F32),
            pltpu.VMEM((NZ - 1, NY, SLAB, HD), F32),
            pltpu.VMEM((NY - 1, NZ, SLAB, HD), F32),
            pltpu.VMEM((2, NY, SLAB, HD), F32),
            pltpu.VMEM((2, NY - 1, SLAB, HD), F32),
            pltpu.VMEM((NX, 4, 2 * HD), F32),
            pltpu.VMEM((NX - 1, 4, 2 * HD), F32),
            pltpu.VMEM((NX, GRAN, chunk, per * 2 * TILE), BF16),
            pltpu.VMEM((NX - 1, GRAN, chunk, per * 2 * TILE), BF16),
            pltpu.VMEM((NX, chunk, hid), BF16),
            pltpu.VMEM((NC, NZ, NY, SLAB, d_dev), BF16),
            pltpu.VMEM((NZ, NY, SLAB, d_dev), BF16),
            pltpu.VMEM((NZ, NY, SLAB, d_dev), BF16),
            pltpu.VMEM((NZ - 1, NY, SLAB, half), BF16),
            pltpu.VMEM((NY - 1, NZ, SLAB, half), BF16),
            pltpu.VMEM((NY, SLAB, half), BF16),
            pltpu.VMEM((NZ, SLAB, half), BF16),
            pltpu.VMEM((NY - 1, SLAB, half), BF16),
            pltpu.VMEM((NZ - 1, SLAB, half), BF16),
            pltpu.VMEM((NX, 4, d_dev), F32),
            pltpu.VMEM((NX, 4, d_dev), F32),
            pltpu.VMEM((batch, HEADS, 128), F32),
            pltpu.VMEM((batch, HEADS, 128), F32),
            pltpu.VMEM((batch, HEADS, HD), F32),
            pltpu.SemaphoreType.DMA((96,)),
            pltpu.SemaphoreType.DMA((96,)),
            pltpu.SemaphoreType.DMA((5, n_tiles)),
        ],
        compiler_params=pltpu.CompilerParams(
            collective_id=0, has_side_effects=True, vmem_limit_bytes=60 << 20
        ),
    )(
        tokens, gain.reshape(1, -1), queries.reshape(batch, HEADS, HD), lengths, w_kv[0],
        w_gate, w_up, w_down, key_cache, value_cache,
    )
    return mixed, context.reshape(batch, HEADS * HD)


def solution(mesh):
    return jax.shard_map(
        body,
        mesh=mesh,
        in_specs=(
            P(("gx", "gy"), None),
            P(),
            P("gy", "gx"),
            P("gy", "gx"),
            P("gx", "gy"),
            P("gy", "gx", None),
            P(("gx", "gy"), None),
            P(("gx", "gy"), None, None),
            P(("gx", "gy"), None, None),
            P(("gx", "gy")),
        ),
        out_specs=(P(("gx", "gy"), None), P(("gx", "gy"), None)),
        check_vma=False,
    )
```

time: 306 us -> 101 us (0.33)
  waiting for transfers between devices: 230 us -> 0 us
  Pallas kernels: 0 us -> 94.5 us
  matrix products: 26.5 us -> 0 us
  between operations: 13.8 us -> 0.64 us
  other arithmetic: 9.81 us -> 0 us
  blocking collectives: 9.16 us -> 0 us
  starting transfers between devices: 8.33 us -> 0 us
    psum x1 -> x0, waiting for transfers between devices: 99.8 us -> none  [body(): summed = lax.psum(pair, 'gy')]
    pallas_call x0 -> x1, Pallas kernels: none -> 94.5 us  [body(): pl.pallas_call(step_kernel, name='step', out_shape=(jax.ShapeDtypeStruct(...]
    reduce_scatter x1 -> x0, waiting for transfers between devices: 83.2 us -> none  [body(): lax.psum_scatter(jnp.concatenate((jnp.dot(hidden, w_down, preferred_eleme...]
    all_gather x1 -> x0, waiting for transfers between devices: 46.8 us -> none  [body(): piece = lax.all_gather(grid_in, 'gx', axis=0, tiled=True)]
    dot_general x7 -> x0, matrix products: 26.5 us -> none  [the longest x1 6.92 us: body(): jnp.dot(hidden, w_down, preferred_element_type=jnp.float32)]
    all_to_all x1 -> x0, blocking collectives: 9.16 us -> none  [body(): lax.all_to_all(normed, 'gy', split_axis=1, concat_axis=0, tiled=True)]
    all_to_all x2 -> x0, starting transfers between devices: 8.21 us -> none  [the longest x1 4.24 us: body(): lax.all_to_all(back[:, :width_dev], 'gy', split_axis=0, concat_axis=1, ti...]
    concatenate x2 -> x0, other arithmetic: 5.4 us -> none  [the longest x1 2.87 us: body(): jnp.concatenate((jnp.dot(hidden, w_down, preferred_element_type=jnp.float...]
  transfers between devices with their start and end apart: 5 -> 0, of which waited for: 4 -> 0; matrix products, arithmetic and copies ran while one was open for 3% -> 0% of each run, Pallas kernels for 0% -> 0%
where the time goes in v1:
time: 101 us; the launch traced here: 99.8 us
  Pallas kernels  94.5 us (94%)
  local copies, waits for them, and re-layouts  4.67 us (5%)
    pallas_call x1, Pallas kernels, body(): pl.pallas_call(step_kernel, name='step', out_shape=(jax.ShapeDtypeStruct(...  94.5 us
    unnamed x3, local copies, waits for them, and re-layouts  4.67 us

profile of v1, /device:TPU:1, one launch (start us, length us, event | category | flops | bytes accessed | tf_op | source)
XLA Modules:
  0.0 99.8 jit_solution(5633129608375616710)
XLA Ops:
  0.6 1.5 %copy.15 = bf16[1,4,48,256]{3,2,1,0:T(8,128)(2,1)} copy(bf16[1,4,48,256]{3,1,2,0:T(4,128)(2,1)} %bitcast.9) | data formatting | bytes 196608
  2.2 94.5 %step.1 = (bf16[4,9216]{1,0:T(4,128)(2,1)}, bf16[4,48,256]{2,1,0:T(8,128)(2,1)}) custom-call(bf16[4,9216]{1,0:T(4,128)(2,1)} %tokens_ref.1, f32[1,9216]{1,0:T(1,128)} %bitcast.13, bf16[4,48,256]{2,1,0:T(8,128)(2,1)} %bitcast.8, s32[4]{0:T(128)} %len_ref.1, bf16[72,512]{1,0:T(8,128)(2,1)} %bitcast.12, bf16[2304,1152]{1,0:T(8,128)(2,1)} %wg_hbm.1, ...), custom_call_target="tpu_custom_call" | custom-call | tf_op jit(solution)/shard_map/step/pallas_call | solution.py:319
  96.7 1.6 %copy.13 = bf16[1,4,48,256]{3,1,2,0:T(4,128)(2,1)} copy(bf16[1,4,48,256]{3,2,1,0:T(8,128)(2,1)} %bitcast.11) | data formatting | bytes 196608
  98.3 1.5 %copy.17 = bf16[4,9216]{1,0:T(4,128)(2,1)} copy(bf16[4,9216]{1,0:T(4,128)(2,1)} %get-tuple-element.8) | data formatting | bytes 147456

commit v2 on v1

v2 whole, which is shorter than its diff:
```python
import functools
import math

import jax
import jax.numpy as jnp
from jax import lax
from jax.experimental import pallas as pl
from jax.experimental.pallas import tpu as pltpu
from jax.sharding import PartitionSpec as P

MESH = pl.DeviceIdType.MESH
HD = 256
HEADS = 48
NZ, NY, NC, NX = 4, 4, 2, 4
SLAB = 16
TILE = 128
GRAN = 3
GRP = 3
F32 = jnp.float32
BF16 = jnp.bfloat16


def step_kernel(
    tokens_ref, gain_ref, q_ref, len_ref, wkv_ref,
    wg_hbm, wu_hbm, wd_hbm, k_hbm, v_hbm,
    ffn_ref, ctx_ref,
    kbuf, vbuf, wgu, wd, nx, xr, xa, wpad, kp, kr, ks, kzr, kyr, kts, kt2r, kx, kxr,
    ps, rf, rn, hs, own, dp, dr, ds_, azr, byr, ta, tb, tar, tbr, fx, fxr,
    q_s, c_s, m_s, l_s, acc_s, ssem, rsem, lsem,
):
    d_dev = xa.shape[-1]
    half = d_dev // 2
    gx = lax.axis_index("gx")
    x = lax.axis_index("gy")
    z = gx // (NY * NC)
    y = lax.rem(gx // NC, NY)
    c = lax.rem(gx, NC)
    oc = 1 - c

    def dev(dz=0, dy=0, dc=0, dx=0):
        zz, yy, cc = lax.rem(z + dz, NZ), lax.rem(y + dy, NY), lax.rem(c + dc, NC)
        return ((zz * NY + yy) * NC + cc, lax.rem(x + dx, NX))

    counter = [0]
    sent = []

    def rcopy(src, dst, device):
        i = counter[0]
        counter[0] += 1
        cp = pltpu.make_async_remote_copy(
            src_ref=src, dst_ref=dst, send_sem=ssem.at[i], recv_sem=rsem.at[i],
            device_id=device, device_id_type=MESH,
        )
        cp.start()
        sent.append(cp)
        return cp

    def arrive(cps):
        for cp in cps:
            cp.wait_recv()

    bar = pltpu.get_barrier_semaphore()
    peers = (
        [dev(dz=i) for i in range(1, NZ)] + [dev(dy=i) for i in range(1, NY)]
        + [dev(dx=i) for i in range(1, NX)] + [dev(dc=1)]
    )
    for peer in peers:
        pl.semaphore_signal(bar, inc=1, device_id=peer, device_id_type=MESH)

    values = tokens_ref[...].astype(F32)
    centred = values - jnp.mean(values, axis=-1, keepdims=True)
    spread = jnp.mean(centred * centred, axis=-1, keepdims=True)
    normed = centred * lax.rsqrt(spread + 1e-05) * gain_ref[...]
    for j in range(NX):
        nx[j] = normed[:, j * d_dev : (j + 1) * d_dev]

    pl.semaphore_wait(bar, len(peers))

    cps = [
        rcopy(nx.at[lax.rem(x + i, NX)], xr.at[x], dev(dx=i)) for i in range(1, NX)
    ]
    xr[x] = nx[x]

    kcp = [pltpu.make_async_copy(k_hbm.at[r], kbuf.at[r], lsem.at[0, r]) for r in range(4)]
    vcp = [pltpu.make_async_copy(v_hbm.at[r], vbuf.at[r], lsem.at[1, r]) for r in range(4)]
    for r in range(4):
        kcp[r].start()
        vcp[r].start()
    n_tiles = wgu.shape[0]

    def weight_copies(t):
        cols = pl.ds(pl.multiple_of(t * TILE, TILE), TILE)
        return (
            pltpu.make_async_copy(wg_hbm.at[:, cols], wgu.at[t, :, pl.ds(0, TILE)], lsem.at[2, t]),
            pltpu.make_async_copy(wu_hbm.at[:, cols], wgu.at[t, :, pl.ds(TILE, TILE)], lsem.at[3, t]),
        )

    for t in range(n_tiles):
        for cp in weight_copies(t):
            cp.start()
    wdcp = pltpu.make_async_copy(wd_hbm, wd, lsem.at[4, 0])
    wdcp.start()

    arrive(cps)
    xa[c, z, y] = jnp.concatenate([xr[j] for j in range(NX)], axis=0).astype(BF16)

    ca, cb = pl.ds(0, half), pl.ds(half, half)
    st1 = [
        rcopy(xa.at[c, z, y, :, ca], xa.at[c, z, y, :, ca], dev(dy=i)) for i in range(1, NY)
    ] + [
        rcopy(xa.at[c, z, y, :, cb], xa.at[c, z, y, :, cb], dev(dz=i)) for i in range(1, NZ)
    ]

    scale = 1.0 / math.sqrt(HD)

    def spread_heads(h, _):
        row = q_ref[:, pl.ds(pl.multiple_of(h * HD, HD), HD)].astype(F32)
        for r in range(4):
            q_s[r, pl.ds(h, 1), :] = row[r : r + 1]
        return 0

    lax.fori_loop(0, HEADS, spread_heads, 0)

    def attend(r):
        s = lax.dot_general(
            q_s[r].astype(BF16), kbuf[r], (((1,), (1,)), ((), ())), preferred_element_type=F32
        ) * scale
        live = lax.broadcasted_iota(jnp.int32, s.shape, 1) < len_ref[r]
        s = jnp.where(live, s, -jnp.inf)
        m = jnp.max(s, axis=-1, keepdims=True)
        p = jnp.exp(s - m)
        l = jnp.sum(p, axis=-1, keepdims=True)
        m_s[r] = jnp.broadcast_to(m, m_s.shape[1:])
        l_s[r] = jnp.broadcast_to(l, l_s.shape[1:])
        acc_s[r] = jnp.dot(p.astype(BF16), vbuf[r], preferred_element_type=F32)

    arrive(st1)
    st2 = [
        rcopy(xa.at[c, z, :, :, ca], xa.at[c, z, :, :, ca], dev(dz=i)) for i in range(1, NZ)
    ] + [
        rcopy(xa.at[c, :, y, :, cb], xa.at[c, :, y, :, cb], dev(dy=i)) for i in range(1, NY)
    ]
    for r in range(4):
        kcp[r].wait()
        vcp[r].wait()
    lax.fori_loop(0, 4, lambda r, _: (attend(r), 0)[1], 0)

    span = wkv_ref.shape[0]
    offset = gx * span
    start = jnp.minimum(offset // TILE, d_dev // TILE - 2) * TILE
    wide = jnp.concatenate(
        [wkv_ref[...].astype(F32), jnp.zeros((2 * TILE - span, 2 * HD), F32)], axis=0
    )
    wpad[...] = pltpu.roll(wide, offset - start, axis=0).astype(BF16)

    arrive(st2)
    sib = rcopy(xa.at[c], xa.at[c], dev(dc=1))

    blk = NZ * NY * SLAB
    rows = NC * blk

    def reduce_core(mine, other, out):
        def add(i, _):
            a, b = i // NY, lax.rem(i, NY)
            out[a, b] = (mine[a, b].astype(F32) + other[a, b].astype(F32)).astype(out.dtype)
            return 0

        lax.fori_loop(0, NZ * NY, add, 0)

    def reduce_first(out, az, by, ha, hb):
        return [
            rcopy(out.at[lax.rem(z + i, NZ), :, :, ha], az.at[i - 1], dev(dz=i)) for i in range(1, NZ)
        ] + [
            rcopy(out.at[:, lax.rem(y + i, NY), :, hb], by.at[i - 1], dev(dy=i)) for i in range(1, NY)
        ]

    def reduce_second(out, az, by, ta, tb, tar, tbr, ha, hb):
        def add_a(b, _):
            total = out[z, b, :, ha].astype(F32)
            for i in range(NZ - 1):
                total += az[i, b].astype(F32)
            ta[b] = total.astype(ta.dtype)
            return 0

        def add_b(a, _):
            total = out[a, y, :, hb].astype(F32)
            for i in range(NY - 1):
                total += by[i, a].astype(F32)
            tb[a] = total.astype(tb.dtype)
            return 0

        lax.fori_loop(0, NY, add_a, 0)
        cps = [rcopy(ta.at[lax.rem(y + i, NY)], tar.at[i - 1], dev(dy=i)) for i in range(1, NY)]
        lax.fori_loop(0, NZ, add_b, 0)
        return cps + [rcopy(tb.at[lax.rem(z + i, NZ)], tbr.at[i - 1], dev(dz=i)) for i in range(1, NZ)]

    def reduce_last(ta, tb, tar, tbr):
        a, b = ta[y].astype(F32), tb[z].astype(F32)
        for i in range(NY - 1):
            a += tar[i].astype(F32)
        for i in range(NZ - 1):
            b += tbr[i].astype(F32)
        return a, b

    per = n_tiles // GRAN
    chunk = blk // NX
    part_rows = chunk // 2
    upper, lower = pl.ds(0, part_rows), pl.ds(part_rows, part_rows)
    right, left = dev(dx=1), dev(dx=NX - 1)
    xp, xm, xf = lax.rem(x + 1, NX), lax.rem(x + NX - 1, NX), lax.rem(x + 2, NX)

    def gate_up(u):
        b, g = divmod(u, GRAN)
        block = c if b == 0 else oc

        def tile(t, _):
            col = pl.ds(pl.multiple_of(t * 2 * TILE, 2 * TILE), 2 * TILE)
            if b == 0:
                for cp in weight_copies(g * per + t):
                    cp.wait()
            part = jnp.dot(
                xa[block].reshape(blk, d_dev), wgu[g * per + t], preferred_element_type=F32
            )
            for k in range(NX):
                ps[u, k, :, col] = part[k * chunk : (k + 1) * chunk].astype(BF16)
            return 0

        lax.fori_loop(0, per, tile, 0)
        far = [
            rcopy(ps.at[u, xf, upper], rf.at[u, 0], right),
            rcopy(ps.at[u, xf, lower], rf.at[u, 1], left),
        ]
        near = [
            rcopy(ps.at[u, xp, lower], rn.at[u, 0, lower], right),
            rcopy(ps.at[u, xm, upper], rn.at[u, 1, upper], left),
        ]
        return far, near

    def pass_on(u, far):
        out = []
        for i, (k, part, device) in enumerate(((xp, upper, right), (xm, lower, left))):
            far[i].wait_recv()
            ps[u, k, part] = (ps[u, k, part].astype(F32) + rf[u, i].astype(F32)).astype(BF16)
            out.append(rcopy(ps.at[u, k, part], rn.at[u, i, part], device))
        return out

    def activate(u, cps):
        b, g = divmod(u, GRAN)
        arrive(cps)
        for t in range(per):
            col = pl.ds(t * 2 * TILE, 2 * TILE)
            total = ps[u, x, :, col].astype(F32)
            for i in range(2):
                total += rn[u, i, :, col].astype(F32)
            gate, up = total[:, :TILE], total[:, TILE:]
            hs[b, x, :, pl.ds((g * per + t) * TILE, TILE)] = (
                gate / (1.0 + jnp.exp(-gate)) * up
            ).astype(BF16)
        cols = pl.ds(g * per * TILE, per * TILE)
        return [
            rcopy(hs.at[b, x, :, cols], hs.at[b, x, :, cols], right),
            rcopy(hs.at[b, x, :, cols], hs.at[b, x, :, cols], left),
        ]

    def forward(u, cps):
        b, g = divmod(u, GRAN)
        cols = pl.ds(g * per * TILE, per * TILE)
        out = []
        for cp, k, part, device in zip(cps, (xm, xp), (upper, lower), (right, left)):
            cp.wait_recv()
            out.append(rcopy(hs.at[b, k, part, cols], hs.at[b, k, part, cols], device))
        return out

    grp_cols = d_dev // GRP

    def down(b, grp):
        into = own if b == 0 else dp

        def tile(t, _):
            src = pl.ds(pl.multiple_of(grp * grp_cols + t * 256, 256), 256)
            dst = pl.ds(pl.multiple_of(t * 256, 256), 256)
            part = jnp.dot(hs[b].reshape(blk, -1), wd[:, src], preferred_element_type=F32)
            into[grp, :, :, :, dst] = part.astype(into.dtype).reshape(NZ, NY, SLAB, 256)
            return 0

        lax.fori_loop(0, grp_cols // 256, tile, 0)

    units = NC * GRAN
    far, near, passed, sent_h, fwd = {}, {}, {}, {}, {}

    def s0(u):
        far[u], near[u] = gate_up(u)

    def s1(u):
        passed[u] = pass_on(u, far[u])

    def s2(u):
        sent_h[u] = activate(u, near[u] + passed[u])

    def s3(u):
        fwd[u] = forward(u, sent_h[u])

    s0(0)
    s0(1)
    s1(0)
    s0(2)
    s1(1)
    sib.wait_recv()

    ka, kb = pl.ds(0, HD), pl.ds(HD, HD)
    xwin = xa[:, :, :, :, pl.ds(pl.multiple_of(start, TILE), 2 * TILE)].reshape(rows, 2 * TILE)
    kp[...] = jnp.dot(xwin, wpad[...], preferred_element_type=F32).reshape(kp.shape)
    kv_core = rcopy(kp.at[oc], kr, dev(dc=1))

    s0(3)
    s1(2)
    kv_core.wait_recv()
    reduce_core(kp.at[c], kr, ks)
    kv1 = reduce_first(ks, kzr, kyr, ka, kb)
    s2(0)
    s0(4)
    s1(3)
    s2(1)
    s3(0)
    arrive(kv1)
    kv2 = reduce_second(
        ks, kzr, kyr, kts.at[0], kts.at[1], kt2r.at[0], kt2r.at[1], ka, kb
    )
    s0(5)
    s1(4)
    s2(2)
    s3(1)
    arrive(kv2)
    key_sum, value_sum = reduce_last(kts.at[0], kts.at[1], kt2r.at[0], kt2r.at[1])
    for j in range(NX):
        kx[j] = jnp.concatenate([key_sum[4 * j : 4 * j + 4], value_sum[4 * j : 4 * j + 4]], axis=1)
    kv3 = [rcopy(kx.at[lax.rem(x + i, NX)], kxr.at[i - 1], dev(dx=i)) for i in range(1, NX)]
    s1(5)
    s2(3)
    s3(2)
    arrive(kv3)
    fresh = kx[x]
    for i in range(NX - 1):
        fresh += kxr[i]
    fresh = fresh.astype(BF16).astype(F32)
    for r in range(4):
        key_new, value_new = fresh[r : r + 1, :HD], fresh[r : r + 1, HD:]
        s_new = jnp.sum(q_s[r] * key_new, axis=-1, keepdims=True) * scale
        m_old = m_s[r][:, :1]
        m = jnp.maximum(m_old, s_new)
        keep, mine = jnp.exp(m_old - m), jnp.exp(s_new - m)
        total = l_s[r][:, :1] * keep + mine
        prob = (mine / total).astype(BF16).astype(F32)
        c_s[r] = acc_s[r] * (keep / total) + prob * value_new

    s2(4)
    s3(3)

    def gather_heads(h, _):
        row = jnp.concatenate([c_s[r, pl.ds(h, 1), :] for r in range(4)], axis=0)
        ctx_ref[:, pl.ds(pl.multiple_of(h * HD, HD), HD)] = row
        return 0

    lax.fori_loop(0, HEADS, gather_heads, 0)
    wdcp.wait()
    arrive(fwd[0] + fwd[1] + fwd[2])
    down(0, 0)
    s2(5)
    s3(4)
    down(0, 1)
    s3(5)
    down(0, 2)
    arrive(fwd[3] + fwd[4] + fwd[5])

    ga, gb = pl.ds(0, grp_cols // 2), pl.ds(grp_cols // 2, grp_cols // 2)
    core, r1, r2 = [], [], []

    def first(i):
        core[i].wait_recv()
        reduce_core(own.at[i], dr.at[i], ds_.at[i])
        r1.append(reduce_first(ds_.at[i], azr.at[i], byr.at[i], ga, gb))

    for i in range(GRP):
        down(1, i)
        core.append(rcopy(dp.at[i], dr.at[i], dev(dc=1)))
        if i:
            first(i - 1)
    first(GRP - 1)
    for i in range(GRP):
        arrive(r1[i])
        r2.append(reduce_second(
            ds_.at[i], azr.at[i], byr.at[i], ta.at[i], tb.at[i], tar.at[i], tbr.at[i], ga, gb
        ))
    for i in range(GRP):
        arrive(r2[i])
        low, high = reduce_last(ta.at[i], tb.at[i], tar.at[i], tbr.at[i])
        for j in range(NX):
            fx[j, :, pl.ds(i * grp_cols, grp_cols // 2)] = low[4 * j : 4 * j + 4]
            fx[j, :, pl.ds(i * grp_cols + grp_cols // 2, grp_cols // 2)] = high[4 * j : 4 * j + 4]
    r3 = [rcopy(fx.at[lax.rem(x + i, NX)], fxr.at[x], dev(dx=i)) for i in range(1, NX)]
    fxr[x] = fx[x]
    arrive(r3)
    for j in range(NX):
        ffn_ref[:, pl.ds(j * d_dev, d_dev)] = fxr[j]
    for cp in sent:
        cp.wait_send()


def body(tokens, gain, w_gate, w_up, w_down, w_kv, queries, key_cache, value_cache, lengths):
    batch, width = tokens.shape
    d_dev, hid = w_gate.shape
    span = key_cache.shape[1]
    n_tiles = hid // TILE
    blk = NZ * NY * SLAB
    chunk = blk // NX
    per = n_tiles // GRAN
    units = NC * GRAN
    gc = d_dev // GRP
    vm = pl.BlockSpec(memory_space=pltpu.VMEM)
    hbm = pl.BlockSpec(memory_space=pltpu.HBM)
    ffn, context = pl.pallas_call(
        step_kernel,
        name="step",
        out_shape=(
            jax.ShapeDtypeStruct((batch, width), F32),
            jax.ShapeDtypeStruct((batch, HEADS * HD), F32),
        ),
        in_specs=[vm, vm, vm, pl.BlockSpec(memory_space=pltpu.SMEM), vm] + [hbm] * 5,
        out_specs=(vm, vm),
        scratch_shapes=[
            pltpu.VMEM((batch, span, HD), BF16),
            pltpu.VMEM((batch, span, HD), BF16),
            pltpu.VMEM((n_tiles, d_dev, 2 * TILE), BF16),
            pltpu.VMEM((hid, d_dev), BF16),
            pltpu.VMEM((NX, 4, d_dev), F32),
            pltpu.VMEM((NX, 4, d_dev), F32),
            pltpu.VMEM((NC, NZ, NY, SLAB, d_dev), BF16),
            pltpu.VMEM((2 * TILE, 2 * HD), BF16),
            pltpu.VMEM((NC, NZ, NY, SLAB, 2 * HD), F32),
            pltpu.VMEM((NZ, NY, SLAB, 2 * HD), F32),
            pltpu.VMEM((NZ, NY, SLAB, 2 * HD), F32),
            pltpu.VMEM((NZ - 1, NY, SLAB, HD), F32),
            pltpu.VMEM((NY - 1, NZ, SLAB, HD), F32),
            pltpu.VMEM((2, NY, SLAB, HD), F32),
            pltpu.VMEM((2, NY - 1, SLAB, HD), F32),
            pltpu.VMEM((NX, 4, 2 * HD), F32),
            pltpu.VMEM((NX - 1, 4, 2 * HD), F32),
            pltpu.VMEM((units, NX, chunk, per * 2 * TILE), BF16),
            pltpu.VMEM((units, 2, chunk // 2, per * 2 * TILE), BF16),
            pltpu.VMEM((units, 2, chunk, per * 2 * TILE), BF16),
            pltpu.VMEM((NC, NX, chunk, hid), BF16),
            pltpu.VMEM((GRP, NZ, NY, SLAB, gc), F32),
            pltpu.VMEM((GRP, NZ, NY, SLAB, gc), BF16),
            pltpu.VMEM((GRP, NZ, NY, SLAB, gc), BF16),
            pltpu.VMEM((GRP, NZ, NY, SLAB, gc), BF16),
            pltpu.VMEM((GRP, NZ - 1, NY, SLAB, gc // 2), BF16),
            pltpu.VMEM((GRP, NY - 1, NZ, SLAB, gc // 2), BF16),
            pltpu.VMEM((GRP, NY, SLAB, gc // 2), BF16),
            pltpu.VMEM((GRP, NZ, SLAB, gc // 2), BF16),
            pltpu.VMEM((GRP, NY - 1, SLAB, gc // 2), BF16),
            pltpu.VMEM((GRP, NZ - 1, SLAB, gc // 2), BF16),
            pltpu.VMEM((NX, 4, d_dev), F32),
            pltpu.VMEM((NX, 4, d_dev), F32),
            pltpu.VMEM((batch, HEADS, HD), F32),
            pltpu.VMEM((batch, HEADS, HD), F32),
            pltpu.VMEM((batch, HEADS, 128), F32),
            pltpu.VMEM((batch, HEADS, 128), F32),
            pltpu.VMEM((batch, HEADS, HD), F32),
            pltpu.SemaphoreType.DMA((144,)),
            pltpu.SemaphoreType.DMA((144,)),
            pltpu.SemaphoreType.DMA((5, n_tiles)),
        ],
        compiler_params=pltpu.CompilerParams(
            collective_id=0, has_side_effects=True, vmem_limit_bytes=60 << 20
        ),
    )(
        tokens, gain.reshape(1, -1), queries, lengths, w_kv[0],
        w_gate, w_up, w_down, key_cache, value_cache,
    )
    mixed = (tokens.astype(F32) + ffn).astype(BF16)
    return mixed, context.astype(BF16)


def solution(mesh):
    return jax.shard_map(
        body,
        mesh=mesh,
        in_specs=(
            P(("gx", "gy"), None),
            P(),
            P("gy", "gx"),
            P("gy", "gx"),
            P("gx", "gy"),
            P("gy", "gx", None),
            P(("gx", "gy"), None),
            P(("gx", "gy"), None, None),
            P(("gx", "gy"), None, None),
            P(("gx", "gy")),
        ),
        out_specs=(P(("gx", "gy"), None), P(("gx", "gy"), None)),
        check_vma=False,
    )
```

time: 101 us -> 88.8 us (0.88)
  Pallas kernels: 94.5 us -> 84 us
  local copies, waits for them, and re-layouts: 4.67 us -> 0.01 us
  other arithmetic: 0 us -> 3.18 us
    pallas_call x1, Pallas kernels: 94.5 us -> 84 us  [body(): pl.pallas_call(step_kernel, name='step', out_shape=(jax.ShapeDtypeStruct(...]
    unnamed x3 -> x2, local copies, waits for them, and re-layouts: 4.67 us -> 0.01 us
    convert_element_type x0 -> x2, other arithmetic: none -> 3.18 us  [the longest x1 1.6 us: body(): return (mixed, context.astype(BF16))]
where the time goes in v2:
time: 88.8 us; the launch traced here: 87.9 us
  Pallas kernels  84 us (95%)
  other arithmetic  3.18 us (4%)
    pallas_call x1, Pallas kernels, body(): pl.pallas_call(step_kernel, name='step', out_shape=(jax.ShapeDtypeStruct(...  84 us

profile of v2, /device:TPU:1, one launch (start us, length us, event | category | flops | bytes accessed | tf_op | source)
XLA Modules:
  0.0 87.9 jit_solution(5350099499944229634)
XLA Ops:
  0.6 0.0 copy-start
  0.6 84.0 %step.1 = (f32[4,9216]{1,0:T(4,128)}, f32[4,12288]{1,0:T(4,128)}) custom-call(bf16[4,9216]{1,0:T(4,128)(2,1)} %tokens_ref.1, f32[1,9216]{1,0:T(1,128)} %bitcast.3, bf16[4,12288]{1,0:T(4,128)(2,1)} %q_ref.1, s32[4]{0:T(128)} %len_ref.1, bf16[72,512]{1,0:T(8,128)(2,1)} %bitcast.2, bf16[2304,1152]{1,0:T(8,128)(2,1)} %wg_hbm.1, bf16[2304,1152]{1,0:T(8,128)(2,1)} %wu_hbm.1, ...), custom_call_target="tpu_custom_call" | custom-call | tf_op jit(solution)/shard_map/step/pallas_call | solution.py:421
  84.7 0.0 copy-done
  84.7 1.6 %add_convert_fusion = bf16[4,9216]{1,0:T(4,128)(2,1)} fusion(f32[4,9216]{1,0:T(4,128)} %get-tuple-element.4, bf16[4,9216]{1,0:T(4,128)(2,1)S(1)} %copy-done), kind=kLoop, calls=%fused_computation | loop fusion | flops 110592 | bytes 294912 | tf_op jit(solution)/shard_map/convert_element_type | solution.py:480
  86.3 1.6 %convert_element_type.11 = bf16[4,12288]{1,0:T(4,128)(2,1)} convert(f32[4,12288]{1,0:T(4,128)} %get-tuple-element.5) | non-fusion elementwise | flops 49152 | bytes 294912 | tf_op jit(solution)/shard_map/convert_element_type | solution.py:481
Async XLA Ops:
  0.6 84.0 %copy-start = (bf16[4,9216]{1,0:T(4,128)(2,1)S(1)}, bf16[4,9216]{1,0:T(4,128)(2,1)}, u32[]{:S(2)}) copy-start(bf16[4,9216]{1,0:T(4,128)(2,1)} %tokens_ref.1) | copy-start | bytes 221188

commit v3 on v2

v3 whole, which is shorter than its diff:
```python
import functools
import math

import jax
import jax.numpy as jnp
from jax import lax
from jax.experimental import pallas as pl
from jax.experimental.pallas import tpu as pltpu
from jax.sharding import PartitionSpec as P

MESH = pl.DeviceIdType.MESH
HD = 256
HEADS = 48
NZ, NY, NC, NX = 4, 4, 2, 4
SLAB = 16
TILE = 128
GRAN = 3
F32 = jnp.float32
BF16 = jnp.bfloat16


def step_kernel(
    len_ref, tok_hbm, gain_hbm, q_hbm, wkv_hbm, wg_hbm, wu_hbm, wd_hbm, k_hbm, v_hbm,
    ffn_ref, ctx_ref,
    tokens_ref, gain_ref, q_ref, wkv_ref,
    kbuf, vbuf, wgu, wd, nx, xr, xa, wpad, kp, kr, ks, kz, kt, ktr, kx, kxr,
    ps, rf, rn, hs, own, dp, dr, ds_, az, tt, tr, fx, fr,
    q_s, c_s, m_s, l_s, acc_s, ssem, rsem, lsem,
):
    d_dev = xa.shape[-1]
    half = d_dev // 2
    gx = lax.axis_index("gx")
    x = lax.axis_index("gy")
    z = gx // (NY * NC)
    y = lax.rem(gx // NC, NY)
    c = lax.rem(gx, NC)
    oc = 1 - c

    def at(zz, yy, cc, xx):
        return ((zz * NY + yy) * NC + cc, xx)

    def dev(dz=0, dy=0, dx=0):
        return at(lax.rem(z + dz, NZ), lax.rem(y + dy, NY), c, lax.rem(x + dx, NX))

    sibling = at(z, y, oc, x)
    gather_first = [dev(dy=i * oc, dz=i * c) for i in range(1, NZ)]
    gather_second = [dev(dz=i * oc, dy=i * c) for i in range(1, NZ)]
    fi, si = z * oc + y * c, y * oc + z * c

    send_count, recv_count, finals = [0], [0], []

    def recvs(n):
        recv_count[0] += n
        return recv_count[0] - n

    def describe(src, dst, device, si_, ri):
        return pltpu.make_async_remote_copy(
            src_ref=src, dst_ref=dst, send_sem=ssem.at[si_], recv_sem=rsem.at[ri],
            device_id=device, device_id_type=MESH,
        )

    def rcopy(src, dst, device, ri=None):
        i = send_count[0]
        send_count[0] += 1
        cp = describe(src, dst, device, i, recvs(1) if ri is None else ri)
        cp.start()
        finals.append(cp.wait_send)
        return cp

    def arrive(cps):
        for cp in cps:
            cp.wait_recv()

    bar = pltpu.get_barrier_semaphore()
    peers = (
        [dev(dz=i) for i in range(1, NZ)] + [dev(dy=i) for i in range(1, NY)]
        + [at(z, y, h, lax.rem(x + i, NX)) for i in range(1, NX) for h in range(NC)] + [sibling]
    )
    for peer in peers:
        pl.semaphore_signal(bar, inc=1, device_id=peer, device_id_type=MESH)

    small = [
        pltpu.make_async_copy(src, dst, lsem.at[4, 1 + i]) for i, (src, dst) in enumerate(
            ((tok_hbm, tokens_ref), (gain_hbm, gain_ref), (q_hbm, q_ref), (wkv_hbm, wkv_ref))
        )
    ]
    kcp = [pltpu.make_async_copy(k_hbm.at[r], kbuf.at[r], lsem.at[0, r]) for r in range(4)]
    vcp = [pltpu.make_async_copy(v_hbm.at[r], vbuf.at[r], lsem.at[1, r]) for r in range(4)]
    per = wgu.shape[2] // (2 * TILE)
    n_tiles = per * GRAN

    def weight_copies(t):
        cols = pl.ds(t * TILE, TILE)
        g, lo = t // per, t % per * 2 * TILE
        return (
            pltpu.make_async_copy(wg_hbm.at[:, cols], wgu.at[g, :, pl.ds(lo, TILE)], lsem.at[2, t]),
            pltpu.make_async_copy(
                wu_hbm.at[:, cols], wgu.at[g, :, pl.ds(lo + TILE, TILE)], lsem.at[3, t]
            ),
        )

    for cp in small:
        cp.start()
    for r in range(4):
        kcp[r].start()
        vcp[r].start()
    for t in range(n_tiles):
        for cp in weight_copies(t):
            cp.start()
    wdcp = pltpu.make_async_copy(wd_hbm, wd, lsem.at[4, 0])
    wdcp.start()

    small[0].wait()
    small[1].wait()
    values = tokens_ref[...].astype(F32)
    centred = values - jnp.mean(values, axis=-1, keepdims=True)
    spread_of = jnp.mean(centred * centred, axis=-1, keepdims=True)
    normed = centred * lax.rsqrt(spread_of + 1e-05) * gain_ref[...]
    for j in range(NX):
        for h in range(NC):
            lo = j * d_dev + h * half
            nx[h, j] = normed[:, lo : lo + half]

    pl.semaphore_wait(bar, len(peers))

    def spread(src, dst):
        base = recvs(7)
        for h in range(NC):
            for i in range(1, NX):
                to = lax.rem(x + i, NX)
                rcopy(src.at[h, to], dst.at[c, x], at(z, y, h, to), base + c * 3 + i - 1)
        rcopy(src.at[oc, x], dst.at[c, x], sibling, base + 6)
        dst[c, x] = src[c, x]
        out = [
            describe(src.at[0, 0], dst.at[h, lax.rem(x + NX - i, NX)], sibling, 0, base + h * 3 + i - 1)
            for h in range(NC) for i in range(1, NX)
        ]
        return out + [describe(src.at[0, 0], dst.at[oc, x], sibling, 0, base + 6)]

    cps = spread(nx, xr)
    c0, c1 = pl.ds(0, half), pl.ds(half, half)
    ch = pl.ds(pl.multiple_of(c * half, TILE), half)
    och = pl.ds(pl.multiple_of(oc * half, TILE), half)
    arrive(cps)

    def gather1(b):
        xa[b, z, y, :, ch] = jnp.concatenate([xr[b, j] for j in range(NX)], axis=0).astype(BF16)
        return [
            rcopy(xa.at[b, z, y, :, ch], xa.at[b, z, y, :, ch], gather_first[i]) for i in range(NZ - 1)
        ]

    def gather2(b):
        sbase, rbase = send_count[0], recvs(NZ - 1)
        send_count[0] += NZ - 1

        def each(do):
            for core, ref in ((0, xa.at[b, z, :, :, c0]), (1, xa.at[b, :, y, :, c1])):
                @pl.when(c == core)
                def _():
                    for i in range(NZ - 1):
                        do(describe(ref, ref, gather_second[i], sbase + i, rbase + i))

        each(lambda cp: cp.start())
        finals.append(lambda: each(lambda cp: cp.wait_send()))
        return lambda: each(lambda cp: cp.wait_recv())

    def gather3(b):
        return rcopy(xa.at[b, :, :, :, ch], xa.at[b, :, :, :, ch], sibling)

    g1 = [gather1(b) for b in range(NC)]
    scale = 1.0 / math.sqrt(HD)

    def spread_heads(h, _):
        row = q_ref[:, pl.ds(pl.multiple_of(h * HD, HD), HD)].astype(F32)
        for r in range(4):
            q_s[r, pl.ds(h, 1), :] = row[r : r + 1]
        return 0

    def attend(r):
        kcp[r].wait()
        vcp[r].wait()
        s = lax.dot_general(
            q_s[r].astype(BF16), kbuf[r], (((1,), (1,)), ((), ())), preferred_element_type=F32
        ) * scale
        live = lax.broadcasted_iota(jnp.int32, s.shape, 1) < len_ref[r]
        s = jnp.where(live, s, -jnp.inf)
        m = jnp.max(s, axis=-1, keepdims=True)
        p = jnp.exp(s - m)
        l = jnp.sum(p, axis=-1, keepdims=True)
        m_s[r] = jnp.broadcast_to(m, m_s.shape[1:])
        l_s[r] = jnp.broadcast_to(l, l_s.shape[1:])
        acc_s[r] = jnp.dot(p.astype(BF16), vbuf[r], preferred_element_type=F32)

    small[2].wait()
    lax.fori_loop(0, HEADS, spread_heads, 0)
    attend(0)
    attend(1)
    arrive(g1[0])
    g2 = [gather2(0)]
    arrive(g1[1])
    g2.append(gather2(1))
    attend(2)
    attend(3)

    small[3].wait()
    span = wkv_ref.shape[0]
    offset = gx * span
    start = jnp.minimum(offset // TILE, d_dev // TILE - 2) * TILE
    wide = jnp.concatenate(
        [wkv_ref[...].astype(F32), jnp.zeros((2 * TILE - span, 2 * HD), F32)], axis=0
    )
    wpad[...] = pltpu.roll(wide, offset - start, axis=0).astype(BF16)

    g2[0]()
    sib0 = gather3(0)
    sib0.wait_recv()

    blk = NZ * NY * SLAB

    chunk = blk // NX
    part_rows = chunk // 2
    upper, lower = pl.ds(0, part_rows), pl.ds(part_rows, part_rows)
    right, left = dev(dx=1), dev(dx=NX - 1)
    xp, xm, xf = lax.rem(x + 1, NX), lax.rem(x + NX - 1, NX), lax.rem(x + 2, NX)

    def gate_up(u):
        b, g = divmod(u, GRAN)

        if b == 0:
            for t in range(per):
                for cp in weight_copies(g * per + t):
                    cp.wait()
        part = jnp.dot(xa[b].reshape(blk, d_dev), wgu[g], preferred_element_type=F32)
        for k in range(NX):
            ps[u, k] = part[k * chunk : (k + 1) * chunk].astype(BF16)
        far = [
            rcopy(ps.at[u, xf, upper], rf.at[u, 0], right),
            rcopy(ps.at[u, xf, lower], rf.at[u, 1], left),
        ]
        near = [
            rcopy(ps.at[u, xp, lower], rn.at[u, 0, lower], right),
            rcopy(ps.at[u, xm, upper], rn.at[u, 1, upper], left),
        ]
        return far, near

    def pass_on(u, far):
        out = []
        for i, (k, part, device) in enumerate(((xp, upper, right), (xm, lower, left))):
            far[i].wait_recv()
            ps[u, k, part] = (ps[u, k, part].astype(F32) + rf[u, i].astype(F32)).astype(BF16)
            out.append(rcopy(ps.at[u, k, part], rn.at[u, i, part], device))
        return out

    def activate(u, cps):
        b, g = divmod(u, GRAN)
        arrive(cps)
        for t in range(per):
            col = pl.ds(t * 2 * TILE, 2 * TILE)
            total = ps[u, x, :, col].astype(F32)
            for i in range(2):
                total += rn[u, i, :, col].astype(F32)
            gate, up = total[:, :TILE], total[:, TILE:]
            hs[b, x, :, pl.ds((g * per + t) * TILE, TILE)] = (
                gate / (1.0 + jnp.exp(-gate)) * up
            ).astype(BF16)
        cols = pl.ds(g * per * TILE, per * TILE)
        return [
            rcopy(hs.at[b, x, :, cols], hs.at[b, x, :, cols], right),
            rcopy(hs.at[b, x, :, cols], hs.at[b, x, :, cols], left),
        ]

    def forward(u, cps):
        b, g = divmod(u, GRAN)
        cols = pl.ds(g * per * TILE, per * TILE)
        out = []
        for cp, k, part, device in zip(cps, (xm, xp), (upper, lower), (right, left)):
            cp.wait_recv()
            out.append(rcopy(hs.at[b, k, part, cols], hs.at[b, k, part, cols], device))
        return out

    far, near, passed, sent_h, fwd = {}, {}, {}, {}, {}

    def s0(u):
        far[u], near[u] = gate_up(u)

    def s1(u):
        passed[u] = pass_on(u, far[u])

    def s2(u):
        sent_h[u] = activate(u, near[u] + passed[u])

    def s3(u):
        fwd[u] = forward(u, sent_h[u])

    pieces = (((0, half),), ((0, 5 * TILE), (5 * TILE, half - 5 * TILE)))

    def down(b, into, first, lo, width):
        src = pl.ds(pl.multiple_of(first + lo, TILE), width)
        part = jnp.dot(hs[b].reshape(blk, -1), wd[:, src], preferred_element_type=F32)
        into[b, :, :, :, lo : lo + width] = part.astype(into.dtype).reshape(NZ, NY, SLAB, width)

    core, r1, r2 = {}, {}, {}

    def da(b, p):
        lo, width = pieces[b][p]
        cols = pl.ds(lo, width)
        down(b, dp, oc * half, lo, width)
        core[b, p] = rcopy(dp.at[b, :, :, :, cols], dr.at[b, :, :, :, cols], sibling)

    def db(b, p):
        down(b, own, c * half, *pieces[b][p])

    def d1(b, p):
        lo, width = pieces[b][p]
        cols = pl.ds(lo, width)
        core[b, p].wait_recv()

        def add(i, _):
            m, n = i // NY, lax.rem(i, NY)
            ds_[b, m * oc + n * c, n * oc + m * c, :, cols] = (
                own[b, m, n, :, cols] + dr[b, m, n, :, cols].astype(F32)
            ).astype(BF16)
            return 0

        lax.fori_loop(0, NZ * NY, add, 0)
        r1[b, p] = [
            rcopy(
                ds_.at[b, lax.rem(fi + i, NZ), :, :, cols], az.at[b, i - 1, :, :, cols],
                gather_second[i - 1],
            )
            for i in range(1, NZ)
        ]

    def d2(b, p):
        lo, width = pieces[b][p]
        cols = pl.ds(lo, width)
        arrive(r1[b, p])

        def add(i, _):
            total = ds_[b, fi, i, :, cols].astype(F32)
            for k in range(NZ - 1):
                total += az[b, k, i, :, cols].astype(F32)
            tt[b, i, :, cols] = total.astype(BF16)
            return 0

        lax.fori_loop(0, NY, add, 0)
        r2[b, p] = [
            rcopy(
                tt.at[b, lax.rem(si + i, NY), :, cols], tr.at[b, i - 1, :, cols],
                gather_first[i - 1],
            )
            for i in range(1, NY)
        ]

    ffn_base = recvs(7)

    def d3(b):
        for p in range(len(pieces[b])):
            arrive(r2[b, p])
        total = tt[b, si].astype(F32)
        for k in range(NY - 1):
            total += tr[b, k].astype(F32)
        for j in range(NX):
            fx[b, j] = total[4 * j : 4 * j + 4]
        for i in range(1, NX):
            to = lax.rem(x + i, NX)
            rcopy(fx.at[b, to], fr.at[c, x], at(z, y, b, to), ffn_base + c * 3 + i - 1)
        sidx = send_count[0]
        send_count[0] += 1

        def across(do):
            @pl.when(c != b)
            def _():
                do(describe(fx.at[b, x], fr.at[c, x], sibling, sidx, ffn_base + 6))

        across(lambda cp: cp.start())
        finals.append(lambda: across(lambda cp: cp.wait_send()))

        @pl.when(c == b)
        def _():
            fr[c, x] = fx[b, x]

    def kv_start():
        xwin = xa[:, :, :, :, pl.ds(pl.multiple_of(start, TILE), 2 * TILE)]
        xwin = xwin.reshape(NC * blk, 2 * TILE)
        for h in range(NC):
            kp[h] = jnp.dot(
                xwin, wpad[:, h * HD : (h + 1) * HD], preferred_element_type=F32
            ).reshape(kp.shape[1:])
        return rcopy(kp.at[oc], kr, sibling)

    def kv_first():
        kv_core.wait_recv()

        def add(i, _):
            p, q = i // NY, lax.rem(i, NY)
            for b in range(NC):
                ks[p * oc + q * c, b, q * oc + p * c] = kp[c, b, p, q] + kr[b, p, q]
            return 0

        lax.fori_loop(0, NZ * NY, add, 0)
        return [
            rcopy(ks.at[lax.rem(fi + i, NZ)], kz.at[i - 1], gather_second[i - 1])
            for i in range(1, NZ)
        ]

    def kv_second():
        arrive(kv1)
        for j in range(NY):
            kt[j] = ks[fi, :, j] + kz[0, :, j] + kz[1, :, j] + kz[2, :, j]
        return [
            rcopy(kt.at[lax.rem(si + i, NY)], ktr.at[i - 1], gather_first[i - 1])
            for i in range(1, NY)
        ]

    def kv_third():
        arrive(kv2)
        kv_sum = kt[si] + ktr[0] + ktr[1] + ktr[2]
        for b in range(NC):
            for j in range(NX):
                kx[b, j] = kv_sum[b, 4 * j : 4 * j + 4]
        return spread(kx, kxr)

    def merge():
        arrive(kv3)
        key_sum, value_sum = kxr[0, 0], kxr[1, 0]
        for j in range(1, NX):
            key_sum, value_sum = key_sum + kxr[0, j], value_sum + kxr[1, j]
        key_sum, value_sum = (v.astype(BF16).astype(F32) for v in (key_sum, value_sum))
        for r in range(4):
            key_new, value_new = key_sum[r : r + 1], value_sum[r : r + 1]
            s_new = jnp.sum(q_s[r] * key_new, axis=-1, keepdims=True) * scale
            m_old = m_s[r][:, :1]
            m = jnp.maximum(m_old, s_new)
            keep, mine = jnp.exp(m_old - m), jnp.exp(s_new - m)
            total = l_s[r][:, :1] * keep + mine
            prob = (mine / total).astype(BF16).astype(F32)
            c_s[r] = acc_s[r] * (keep / total) + prob * value_new

    def gather_heads(h, _):
        row = jnp.concatenate([c_s[r, pl.ds(h, 1), :] for r in range(4)], axis=0)
        ctx_ref[:, pl.ds(pl.multiple_of(h * HD, HD), HD)] = row
        return 0

    s0(0)
    s0(1)
    s0(2)
    g2[1]()
    sib1 = gather3(1)
    s1(1)
    s1(0)
    sib1.wait_recv()
    kv_core = kv_start()
    s0(3)
    s1(2)
    s2(0)
    kv1 = kv_first()
    s0(4)
    s2(1)
    s2(2)
    s0(5)
    s1(4)
    s1(3)
    s1(5)
    s3(0)
    s3(2)
    s3(1)
    s2(3)
    kv2 = kv_second()
    s2(5)
    s2(4)
    wdcp.wait()
    arrive(fwd[0] + fwd[1] + fwd[2])
    da(0, 0)
    s3(3)
    s3(5)
    s3(4)
    kv3 = kv_third()
    db(0, 0)
    d1(0, 0)
    arrive(fwd[3] + fwd[4] + fwd[5])
    da(1, 1)
    db(1, 1)
    da(1, 0)
    db(1, 0)
    d1(1, 1)
    d1(1, 0)
    merge()
    lax.fori_loop(0, HEADS, gather_heads, 0)
    d2(0, 0)
    d2(1, 1)
    d2(1, 0)
    d3(0)
    d3(1)
    for h in range(NC):
        for i in range(1, NX):
            describe(
                fx.at[0, 0], fr.at[h, lax.rem(x + NX - i, NX)], sibling, 0, ffn_base + h * 3 + i - 1
            ).wait_recv()
    describe(fx.at[0, 0], fr.at[oc, x], sibling, 0, ffn_base + 6).wait_recv()
    for j in range(NX):
        for h in range(NC):
            ffn_ref[:, pl.ds(j * d_dev + h * half, half)] = fr[h, j]
    for wait in finals:
        wait()


def body(tokens, gain, w_gate, w_up, w_down, w_kv, queries, key_cache, value_cache, lengths):
    batch, width = tokens.shape
    d_dev, hid = w_gate.shape
    half = d_dev // 2
    span = key_cache.shape[1]
    n_tiles = hid // TILE
    blk = NZ * NY * SLAB
    chunk = blk // NX
    per = n_tiles // GRAN
    units = NC * GRAN
    vm = pl.BlockSpec(memory_space=pltpu.VMEM)
    hbm = pl.BlockSpec(memory_space=pltpu.HBM)
    ffn, context = pl.pallas_call(
        step_kernel,
        name="step",
        out_shape=(
            jax.ShapeDtypeStruct((batch, width), F32),
            jax.ShapeDtypeStruct((batch, HEADS * HD), F32),
        ),
        in_specs=[pl.BlockSpec(memory_space=pltpu.SMEM)] + [hbm] * 9,
        out_specs=(vm, vm),
        scratch_shapes=[
            pltpu.VMEM((batch, width), BF16),
            pltpu.VMEM((1, width), F32),
            pltpu.VMEM((batch, HEADS * HD), BF16),
            pltpu.VMEM(w_kv.shape[1:], BF16),
            pltpu.VMEM((batch, span, HD), BF16),
            pltpu.VMEM((batch, span, HD), BF16),
            pltpu.VMEM((GRAN, d_dev, per * 2 * TILE), BF16),
            pltpu.VMEM((hid, d_dev), BF16),
            pltpu.VMEM((NC, NX, 4, half), F32),
            pltpu.VMEM((NC, NX, 4, half), F32),
            pltpu.VMEM((NC, NZ, NY, SLAB, d_dev), BF16),
            pltpu.VMEM((2 * TILE, 2 * HD), BF16),
            pltpu.VMEM((NC, NC, NZ, NY, SLAB, HD), F32),
            pltpu.VMEM((NC, NZ, NY, SLAB, HD), F32),
            pltpu.VMEM((NZ, NC, NY, SLAB, HD), F32),
            pltpu.VMEM((NZ - 1, NC, NY, SLAB, HD), F32),
            pltpu.VMEM((NY, NC, SLAB, HD), F32),
            pltpu.VMEM((NY - 1, NC, SLAB, HD), F32),
            pltpu.VMEM((NC, NX, 4, HD), F32),
            pltpu.VMEM((NC, NX, 4, HD), F32),
            pltpu.VMEM((units, NX, chunk, per * 2 * TILE), BF16),
            pltpu.VMEM((units, 2, chunk // 2, per * 2 * TILE), BF16),
            pltpu.VMEM((units, 2, chunk, per * 2 * TILE), BF16),
            pltpu.VMEM((NC, NX, chunk, hid), BF16),
            pltpu.VMEM((NC, NZ, NY, SLAB, half), F32),
            pltpu.VMEM((NC, NZ, NY, SLAB, half), BF16),
            pltpu.VMEM((NC, NZ, NY, SLAB, half), BF16),
            pltpu.VMEM((NC, NZ, NY, SLAB, half), BF16),
            pltpu.VMEM((NC, NZ - 1, NY, SLAB, half), BF16),
            pltpu.VMEM((NC, NY, SLAB, half), BF16),
            pltpu.VMEM((NC, NY - 1, SLAB, half), BF16),
            pltpu.VMEM((NC, NX, 4, half), F32),
            pltpu.VMEM((NC, NX, 4, half), F32),
            pltpu.VMEM((batch, HEADS, HD), F32),
            pltpu.VMEM((batch, HEADS, HD), F32),
            pltpu.VMEM((batch, HEADS, 128), F32),
            pltpu.VMEM((batch, HEADS, 128), F32),
            pltpu.VMEM((batch, HEADS, HD), F32),
            pltpu.SemaphoreType.DMA((144,)),
            pltpu.SemaphoreType.DMA((144,)),
            pltpu.SemaphoreType.DMA((5, n_tiles)),
        ],
        compiler_params=pltpu.CompilerParams(
            collective_id=0, has_side_effects=True, vmem_limit_bytes=60 << 20
        ),
    )(
        lengths, tokens, gain.reshape(1, -1), queries, w_kv[0],
        w_gate, w_up, w_down, key_cache, value_cache,
    )
    mixed = (tokens.astype(F32) + ffn).astype(BF16)
    return mixed, context.astype(BF16)


def solution(mesh):
    return jax.shard_map(
        body,
        mesh=mesh,
        in_specs=(
            P(("gx", "gy"), None),
            P(),
            P("gy", "gx"),
            P("gy", "gx"),
            P("gx", "gy"),
            P("gy", "gx", None),
            P(("gx", "gy"), None),
            P(("gx", "gy"), None, None),
            P(("gx", "gy"), None, None),
            P(("gx", "gy")),
        ),
        out_specs=(P(("gx", "gy"), None), P(("gx", "gy"), None)),
        check_vma=False,
    )
```

time: 88.8 us -> 82.8 us (0.932)
  Pallas kernels: 84 us -> 78.8 us
    pallas_call x1, Pallas kernels: 84 us -> 78.8 us  [body(): pl.pallas_call(step_kernel, name='step', out_shape=(jax.ShapeDtypeStruct(...]
where the time goes in v3:
time: 82.8 us; the launch traced here: 82.6 us
  Pallas kernels  78.8 us (95%)
  other arithmetic  3.18 us (4%)
    pallas_call x1, Pallas kernels, body(): pl.pallas_call(step_kernel, name='step', out_shape=(jax.ShapeDtypeStruct(...  78.8 us

profile of v3, /device:TPU:1, one launch (start us, length us, event | category | flops | bytes accessed | tf_op | source)
XLA Modules:
  0.0 82.6 jit_solution(7165938981961936041)
XLA Ops:
  0.6 0.0 copy-start
  0.6 78.8 %step.1 = (f32[4,9216]{1,0:T(4,128)}, f32[4,12288]{1,0:T(4,128)}) custom-call(s32[4]{0:T(128)} %len_ref.1, bf16[4,9216]{1,0:T(4,128)(2,1)} %tok_hbm.1, f32[1,9216]{1,0:T(1,128)} %bitcast.3, bf16[4,12288]{1,0:T(4,128)(2,1)} %q_hbm.1, bf16[72,512]{1,0:T(8,128)(2,1)} %bitcast.2, bf16[2304,1152]{1,0:T(8,128)(2,1)} %wg_hbm.1, bf16[2304,1152]{1,0:T(8,128)(2,1)} %wu_hbm.1, ...), custom_call_target="tpu_custom_call" | custom-call | tf_op jit(solution)/shard_map/step/pallas_call | solution.py:520
  79.5 0.0 copy-done
  79.5 1.6 %add_convert_fusion = bf16[4,9216]{1,0:T(4,128)(2,1)} fusion(f32[4,9216]{1,0:T(4,128)} %get-tuple-element.4, bf16[4,9216]{1,0:T(4,128)(2,1)S(1)} %copy-done), kind=kLoop, calls=%fused_computation | loop fusion | flops 110592 | bytes 294912 | tf_op jit(solution)/shard_map/convert_element_type | solution.py:579
  81.0 1.6 %convert_element_type.11 = bf16[4,12288]{1,0:T(4,128)(2,1)} convert(f32[4,12288]{1,0:T(4,128)} %get-tuple-element.5) | non-fusion elementwise | flops 49152 | bytes 294912 | tf_op jit(solution)/shard_map/convert_element_type | solution.py:580
Async XLA Ops:
  0.6 78.8 %copy-start = (bf16[4,9216]{1,0:T(4,128)(2,1)S(1)}, bf16[4,9216]{1,0:T(4,128)(2,1)}, u32[]{:S(2)}) copy-start(bf16[4,9216]{1,0:T(4,128)(2,1)} %tok_hbm.1) | copy-start | bytes 221188

commit v4 on v3

--- a/solution.py
+++ b/solution.py
@@ -49,6 +49,10 @@
 
     send_count, recv_count, finals = [0], [0], []
 
+    def sends(n):
+        send_count[0] += n
+        return send_count[0] - n
+
     def recvs(n):
         recv_count[0] += n
         return recv_count[0] - n
@@ -60,12 +64,16 @@
         )
 
     def rcopy(src, dst, device, ri=None):
-        i = send_count[0]
-        send_count[0] += 1
+        i = sends(1)
         cp = describe(src, dst, device, i, recvs(1) if ri is None else ri)
         cp.start()
         finals.append(cp.wait_send)
         return cp
+
+    def drain():
+        for wait in finals:
+            wait()
+        finals.clear()
 
     def arrive(cps):
         for cp in cps:
@@ -140,7 +148,6 @@
     cps = spread(nx, xr)
     c0, c1 = pl.ds(0, half), pl.ds(half, half)
     ch = pl.ds(pl.multiple_of(c * half, TILE), half)
-    och = pl.ds(pl.multiple_of(oc * half, TILE), half)
     arrive(cps)
 
     def gather1(b):
@@ -150,22 +157,51 @@
         ]
 
     def gather2(b):
-        sbase, rbase = send_count[0], recvs(NZ - 1)
-        send_count[0] += NZ - 1
+        sbase, rbase = sends(2 * NZ - 1), recvs(2 * NZ - 1)
+
+        def group(core, i):
+            if core == 0:
+                return xa.at[b, lax.rem(z + NZ - i, NZ), :, :, c0]
+            return xa.at[b, :, lax.rem(y + NY - i, NY), :, c1]
 
         def each(do):
-            for core, ref in ((0, xa.at[b, z, :, :, c0]), (1, xa.at[b, :, y, :, c1])):
+            for core in range(NC):
                 @pl.when(c == core)
                 def _():
-                    for i in range(NZ - 1):
-                        do(describe(ref, ref, gather_second[i], sbase + i, rbase + i))
-
-        each(lambda cp: cp.start())
-        finals.append(lambda: each(lambda cp: cp.wait_send()))
-        return lambda: each(lambda cp: cp.wait_recv())
-
-    def gather3(b):
-        return rcopy(xa.at[b, :, :, :, ch], xa.at[b, :, :, :, ch], sibling)
+                    do(core)
+
+        def out(core, i):
+            ref = group(core, 0)
+            return describe(ref, ref, gather_second[i - 1], sbase + i, rbase + i)
+
+        def over(core, i):
+            ref = group(core, i)
+            k = i + NZ - 1 if i else 0
+            return describe(ref, ref, sibling, sbase + k, rbase + k)
+
+        def begin(core):
+            for i in range(1, NZ):
+                out(core, i).start()
+            over(core, 0).start()
+
+        def onward(core):
+            for i in (1, 3, 2):
+                out(core, i).wait_recv()
+                over(core, i).start()
+
+        def received(core):
+            for i in range(NZ):
+                over(1 - core, i).wait_recv()
+
+        def sent(core):
+            for i in range(1, NZ):
+                out(core, i).wait_send()
+            for i in range(NZ):
+                over(core, i).wait_send()
+
+        each(begin)
+        finals.append(lambda: each(sent))
+        return lambda: each(onward), lambda: each(received)
 
     g1 = [gather1(b) for b in range(NC)]
     scale = 1.0 / math.sqrt(HD)
@@ -211,9 +247,8 @@
     )
     wpad[...] = pltpu.roll(wide, offset - start, axis=0).astype(BF16)
 
-    g2[0]()
-    sib0 = gather3(0)
-    sib0.wait_recv()
+    g2[0][0]()
+    g2[0][1]()
 
     blk = NZ * NY * SLAB
 
@@ -365,8 +400,7 @@
         for i in range(1, NX):
             to = lax.rem(x + i, NX)
             rcopy(fx.at[b, to], fr.at[c, x], at(z, y, b, to), ffn_base + c * 3 + i - 1)
-        sidx = send_count[0]
-        send_count[0] += 1
+        sidx = sends(1)
 
         def across(do):
             @pl.when(c != b)
@@ -445,11 +479,10 @@
     s0(0)
     s0(1)
     s0(2)
-    g2[1]()
-    sib1 = gather3(1)
+    g2[1][0]()
     s1(1)
     s1(0)
-    sib1.wait_recv()
+    g2[1][1]()
     kv_core = kv_start()
     s0(3)
     s1(2)
@@ -487,6 +520,7 @@
     d1(1, 0)
     merge()
     lax.fori_loop(0, HEADS, gather_heads, 0)
+    drain()
     d2(0, 0)
     d2(1, 1)
     d2(1, 0)
@@ -501,8 +535,12 @@
     for j in range(NX):
         for h in range(NC):
             ffn_ref[:, pl.ds(j * d_dev + h * half, half)] = fr[h, j]
-    for wait in finals:
-        wait()
+    drain()
+
+
+def finish_kernel(tokens_ref, ffn_ref, context_ref, mixed_ref, ctx_ref):
+    mixed_ref[...] = (tokens_ref[...].astype(F32) + ffn_ref[...]).astype(BF16)
+    ctx_ref[...] = context_ref[...].astype(BF16)
 
 
 def body(tokens, gain, w_gate, w_up, w_down, w_kv, queries, key_cache, value_cache, lengths):
@@ -576,8 +614,16 @@
         lengths, tokens, gain.reshape(1, -1), queries, w_kv[0],
         w_gate, w_up, w_down, key_cache, value_cache,
     )
-    mixed = (tokens.astype(F32) + ffn).astype(BF16)
-    return mixed, context.astype(BF16)
+    return pl.pallas_call(
+        finish_kernel,
+        name="finish",
+        out_shape=(
+            jax.ShapeDtypeStruct((batch, width), BF16),
+            jax.ShapeDtypeStruct((batch, HEADS * HD), BF16),
+        ),
+        in_specs=[vm, vm, vm],
+        out_specs=(vm, vm),
+    )(tokens, ffn, context)
 
 
 def solution(mesh):

time: 82.8 us -> 79.6 us (0.961)
  other arithmetic: 3.18 us -> 0 us
    convert_element_type x2 -> x0, other arithmetic: 3.18 us -> none  [the longest x1 1.6 us: body(): return (mixed, context.astype(BF16))]
    pallas_call x1, Pallas kernels: 78.8 us -> 77.1 us  [body(): pl.pallas_call(step_kernel, name='step', out_shape=(jax.ShapeDtypeStruct(...]
    pallas_call x0 -> x1, Pallas kernels: none -> 1.73 us  [body(): pl.pallas_call(finish_kernel, name='finish', out_shape=(jax.ShapeDtypeStr...]
where the time goes in v4:
time: 79.6 us; the launch traced here: 79.4 us
  Pallas kernels  78.8 us (99%)
    pallas_call x1, Pallas kernels, body(): pl.pallas_call(step_kernel, name='step', out_shape=(jax.ShapeDtypeStruct(...  77.1 us
    pallas_call x1, Pallas kernels, body(): pl.pallas_call(finish_kernel, name='finish', out_shape=(jax.ShapeDtypeStr...  1.73 us

profile of v4, /device:TPU:1, one launch (start us, length us, event | category | flops | bytes accessed | tf_op | source)
XLA Modules:
  0.0 79.4 jit_solution(14105051870827535452)
XLA Ops:
  0.6 77.1 %step.1 = (f32[4,9216]{1,0:T(4,128)}, f32[4,12288]{1,0:T(4,128)}) custom-call(s32[4]{0:T(128)} %len_ref.1, bf16[4,9216]{1,0:T(4,128)(2,1)} %tokens_ref.1, f32[1,9216]{1,0:T(1,128)} %bitcast.3, bf16[4,12288]{1,0:T(4,128)(2,1)} %q_hbm.1, bf16[72,512]{1,0:T(8,128)(2,1)} %bitcast.2, bf16[2304,1152]{1,0:T(8,128)(2,1)} %wg_hbm.1, bf16[2304,1152]{1,0:T(8,128)(2,1)} %wu_hbm.1, ...), custom_call_target="tpu_custom_call" | custom-call | tf_op jit(solution)/shard_map/step/pallas_call | solution.py:558
  77.7 1.7 %finish.1 = (bf16[4,9216]{1,0:T(4,128)(2,1)}, bf16[4,12288]{1,0:T(4,128)(2,1)}) custom-call(bf16[4,9216]{1,0:T(4,128)(2,1)} %tokens_ref.1, f32[4,9216]{1,0:T(4,128)} %get-tuple-element.4.ffn_ref, f32[4,12288]{1,0:T(4,128)} %get-tuple-element.5.context_ref), custom_call_target="tpu_custom_call" | custom-call | tf_op jit(solution)/shard_map/finish/pallas_call | solution.py:617

commit v5 on v4

--- a/solution.py
+++ b/solution.py
@@ -127,7 +127,7 @@
     for j in range(NX):
         for h in range(NC):
             lo = j * d_dev + h * half
-            nx[h, j] = normed[:, lo : lo + half]
+            nx[h, j] = normed[:, lo : lo + half].astype(BF16)
 
     pl.semaphore_wait(bar, len(peers))
 
@@ -151,7 +151,9 @@
     arrive(cps)
 
     def gather1(b):
-        xa[b, z, y, :, ch] = jnp.concatenate([xr[b, j] for j in range(NX)], axis=0).astype(BF16)
+        xa[b, z, y, :, ch] = jnp.concatenate(
+            [xr[b, j].astype(F32) for j in range(NX)], axis=0
+        ).astype(BF16)
         return [
             rcopy(xa.at[b, z, y, :, ch], xa.at[b, z, y, :, ch], gather_first[i]) for i in range(NZ - 1)
         ]
@@ -513,10 +515,10 @@
     d1(0, 0)
     arrive(fwd[3] + fwd[4] + fwd[5])
     da(1, 1)
+    da(1, 0)
     db(1, 1)
-    da(1, 0)
+    d1(1, 1)
     db(1, 0)
-    d1(1, 1)
     d1(1, 0)
     merge()
     lax.fori_loop(0, HEADS, gather_heads, 0)
@@ -573,8 +575,8 @@
             pltpu.VMEM((batch, span, HD), BF16),
             pltpu.VMEM((GRAN, d_dev, per * 2 * TILE), BF16),
             pltpu.VMEM((hid, d_dev), BF16),
-            pltpu.VMEM((NC, NX, 4, half), F32),
-            pltpu.VMEM((NC, NX, 4, half), F32),
+            pltpu.VMEM((NC, NX, 4, half), BF16),
+            pltpu.VMEM((NC, NX, 4, half), BF16),
             pltpu.VMEM((NC, NZ, NY, SLAB, d_dev), BF16),
             pltpu.VMEM((2 * TILE, 2 * HD), BF16),
             pltpu.VMEM((NC, NC, NZ, NY, SLAB, HD), F32),

time: 79.6 us -> 78.7 us (0.989)
  Pallas kernels: 78.8 us -> 78 us
    pallas_call x1, Pallas kernels: 77.1 us -> 76.2 us  [body(): pl.pallas_call(step_kernel, name='step', out_shape=(jax.ShapeDtypeStruct(...]
where the time goes in v5:
time: 78.7 us; the launch traced here: 78.6 us
  Pallas kernels  78 us (99%)
    pallas_call x1, Pallas kernels, body(): pl.pallas_call(step_kernel, name='step', out_shape=(jax.ShapeDtypeStruct(...  76.2 us
    pallas_call x1, Pallas kernels, body(): pl.pallas_call(finish_kernel, name='finish', out_shape=(jax.ShapeDtypeStr...  1.73 us

profile of v5, /device:TPU:1, one launch (start us, length us, event | category | flops | bytes accessed | tf_op | source)
XLA Modules:
  0.0 78.6 jit_solution(16577577101831339883)
XLA Ops:
  0.6 76.2 %step.1 = (f32[4,9216]{1,0:T(4,128)}, f32[4,12288]{1,0:T(4,128)}) custom-call(s32[4]{0:T(128)} %len_ref.1, bf16[4,9216]{1,0:T(4,128)(2,1)} %tokens_ref.1, f32[1,9216]{1,0:T(1,128)} %bitcast.3, bf16[4,12288]{1,0:T(4,128)(2,1)} %q_hbm.1, bf16[72,512]{1,0:T(8,128)(2,1)} %bitcast.2, bf16[2304,1152]{1,0:T(8,128)(2,1)} %wg_hbm.1, bf16[2304,1152]{1,0:T(8,128)(2,1)} %wu_hbm.1, ...), custom_call_target="tpu_custom_call" | custom-call | tf_op jit(solution)/shard_map/step/pallas_call | solution.py:560
  76.9 1.7 %finish.1 = (bf16[4,9216]{1,0:T(4,128)(2,1)}, bf16[4,12288]{1,0:T(4,128)(2,1)}) custom-call(bf16[4,9216]{1,0:T(4,128)(2,1)} %tokens_ref.1, f32[4,9216]{1,0:T(4,128)} %get-tuple-element.4.ffn_ref, f32[4,12288]{1,0:T(4,128)} %get-tuple-element.5.context_ref), custom_call_target="tpu_custom_call" | custom-call | tf_op jit(solution)/shard_map/finish/pallas_call | solution.py:619
